TPU v7x, 256 devices: a whole 4x4x8 slice. The times are simulated.
256 devices in a mesh: slab: 32 (over x, z), hodlr: 8 (over y, core).
Axes of the slice: x: 4, y: 4, z: 8, core: 2. Of those that a mesh axis runs over, the one named last changes fastest.
Arguments:
- sources: bfloat16 [32, 32, 16384], P('slab', None, 'hodlr'), may hold values from -2 to 2
- leaves: bfloat16 [32, 16, 1024, 1024], P('slab', 'hodlr'), may hold values from -1 to 2
- v_rows: bfloat16 [32, 4, 64, 16384], P('slab', None, None, 'hodlr'), may hold values from -0.0625 to 0.0625
- u_rows: bfloat16 [32, 4, 64, 16384], P('slab', None, None, 'hodlr'), may hold values from -0.1875 to 0.1875
Outputs:
- fronts: bfloat16 [32, 32, 16384], P('slab', None, 'hodlr')
All inputs are finite; a program needn't handle non-finite values.
Results may differ from a plain program's by a relative error of at most 0.025.
Values may be sent and summed in bfloat16 or wider, within the bound.
A program may use at most 64 MiB of HBM per device.

v0:
```python
import jax
import jax.numpy as jnp
from jax import lax
from jax.sharding import PartitionSpec as P


def passed_along(block, axis, distance):
    devices = range(lax.axis_size(axis))
    route = [(i - distance, i) for i in devices if i - distance in devices]
    return lax.ppermute(block, axis, route)


def local(sources, leaves, v_rows, u_rows):
    devices = lax.axis_size("hodlr")
    chain = lax.axis_size("slab")
    position = lax.axis_index("slab")
    member = lax.axis_index("hodlr")
    cross = devices.bit_length() - 1
    source = sources[0]
    leaf = leaves[0]
    right = v_rows[0]
    left = u_rows[0]
    shot_batch, width = source.shape
    rank = right.shape[1]
    nleaf = leaf.shape[0]
    leaf_size = leaf.shape[1]
    peers = jnp.arange(devices, dtype=jnp.int32)
    sibling_rows = []
    for tree_level in range(1, cross + 1):
        group = devices >> tree_level
        sibling_rows.append(
            (peers // group == jnp.bitwise_xor(member // group, 1)).astype(jnp.float32)
        )
    sibling_mask = jnp.stack(sibling_rows)

    def partials_of(w, factors):
        rows = w.shape[0]
        return jnp.einsum("sn,crn->csr", w, factors, preferred_element_type=jnp.float32).reshape(
            cross, rows * rank
        )

    def combine_gathered(gathered, rows):
        sibling = jnp.einsum("pcx,cp->cx", gathered, sibling_mask, precision=lax.Precision.HIGHEST)
        return sibling.reshape(cross, rows, rank).astype(jnp.bfloat16)

    def local_part(w):
        rows = w.shape[0]
        sweep_output = jnp.einsum(
            "sbj,bjo->sbo",
            w.reshape(rows, nleaf, leaf_size),
            leaf,
            preferred_element_type=jnp.float32,
        ).reshape(rows, width)
        block_size = width * devices >> 4
        block_list = width // block_size
        projection_rows = jnp.einsum(
            "kqc,vqc->kqv",
            w.reshape(rows, block_list, block_size),
            right[3].reshape(rank, block_list, block_size),
            preferred_element_type=jnp.float32,
        ).astype(jnp.bfloat16)
        swapped_halves = projection_rows.reshape(rows, block_list // 2, 2, rank)[
            :, :, ::-1
        ].reshape(rows, block_list, rank)
        sweep_output = sweep_output + jnp.einsum(
            "cwp,pwi->cwi",
            swapped_halves,
            left[3].reshape(rank, block_list, block_size),
            preferred_element_type=jnp.float32,
        ).reshape(rows, width)
        return sweep_output

    def finish(sweep_output, sibling):
        sweep_output = sweep_output + jnp.einsum(
            "csr,crn->sn", sibling, left[:cross], preferred_element_type=jnp.float32
        )
        return sweep_output.astype(jnp.bfloat16)

    def apply(w):
        rows = w.shape[0]
        partial_value = partials_of(w, right[:cross])
        sweep_output = local_part(w)
        gathered = lax.all_gather(partial_value[None], "hodlr", axis=0, tiled=True)
        sibling = combine_gathered(gathered, rows)
        return finish(sweep_output, sibling)

    groups = 1
    batch = shot_batch // groups

    def advance(step, carry):
        front, swept = carry
        incoming = passed_along(front, "slab", 1)
        offset = step - position
        valid = (offset >= 0) & (offset < groups)
        w = (source.astype(jnp.float32) + incoming.astype(jnp.float32)).astype(jnp.bfloat16)
        sweep_output = apply(w)
        current = swept
        swept = jnp.where(valid, sweep_output, current)
        return (sweep_output, swept)

    initial = (
        jnp.zeros((batch, width), jnp.bfloat16),
        jnp.zeros((shot_batch, width), jnp.bfloat16),
    )
    _, swept = lax.fori_loop(0, chain + groups - 1, advance, initial)
    return swept[None]


def solution(mesh):
    in_specs = (
        P("slab", None, "hodlr"),
        P("slab", "hodlr", None, None),
        P("slab", None, None, "hodlr"),
        P("slab", None, None, "hodlr"),
    )
    out_specs = P("slab", None, "hodlr")
    return jax.shard_map(local, mesh=mesh, in_specs=in_specs, out_specs=out_specs, check_vma=False)
```

profile of v0, /device:TPU:7, one launch (start us, length us, event | category | flops | bytes accessed | tf_op | source)
XLA Modules:
  0.0 952.1 jit_solution(5715799266085852439)
XLA Ops:
  0.1 951.3 %while.16 = (s32[]{:T(128)}, bf16[32,2048]{1,0:T(8,128)(2,1)S(1)}, bf16[32,2048]{1,0:T(8,128)(2,1)S(1)}, bf16[32,2048]{1,0:T(8,128)(2,1)}, bf16[2,1024,1024]{2,1...) while((s32[]{:T(128)}, bf16[32,2048]{1,0:T(8,128)(2,1)S(1)}, ...), condition=%wide.region_1.2_spmd.clone, body=%wide.region_0.1_spmd.clone.sunk | while | flops 202575872 | bytes 16732478 | solution.py:105
  6.0 5.1 collective-permute-done
  17.2 14.4 %all_gather.9 = f32[8,3,2048]{2,1,0:T(4,128)S(1)} all-gather(f32[1,3,2048]{2,1,0:T(4,128)S(1)} %reshape.133), channel_id=1, replica_groups=mesh['slab'=32,'hodlr'=8] {'hodlr'}, dimensions={0}, use_global_device_ids=true | all-gather | bytes 221184 | tf_op jit(solution)/shard_map/while/body/eval_jaxpr/all_gather | solution.py:83
  36.8 4.6 collective-permute-done
  47.6 13.7 %all_gather.9 = f32[8,3,2048]{2,1,0:T(4,128)S(1)} all-gather(f32[1,3,2048]{2,1,0:T(4,128)S(1)} %reshape.133), channel_id=1, replica_groups=mesh['slab'=32,'hodlr'=8] {'hodlr'}, dimensions={0}, use_global_device_ids=true | all-gather | bytes 221184 | tf_op jit(solution)/shard_map/while/body/eval_jaxpr/all_gather | solution.py:83
  66.4 4.6 collective-permute-done
  77.2 13.7 %all_gather.9 = f32[8,3,2048]{2,1,0:T(4,128)S(1)} all-gather(f32[1,3,2048]{2,1,0:T(4,128)S(1)} %reshape.133), channel_id=1, replica_groups=mesh['slab'=32,'hodlr'=8] {'hodlr'}, dimensions={0}, use_global_device_ids=true | all-gather | bytes 221184 | tf_op jit(solution)/shard_map/while/body/eval_jaxpr/all_gather | solution.py:83
  106.9 13.7 %all_gather.9 = f32[8,3,2048]{2,1,0:T(4,128)S(1)} all-gather(f32[1,3,2048]{2,1,0:T(4,128)S(1)} %reshape.133), channel_id=1, replica_groups=mesh['slab'=32,'hodlr'=8] {'hodlr'}, dimensions={0}, use_global_device_ids=true | all-gather | bytes 221184 | tf_op jit(solution)/shard_map/while/body/eval_jaxpr/all_gather | solution.py:83
  136.5 13.7 %all_gather.9 = f32[8,3,2048]{2,1,0:T(4,128)S(1)} all-gather(f32[1,3,2048]{2,1,0:T(4,128)S(1)} %reshape.133), channel_id=1, replica_groups=mesh['slab'=32,'hodlr'=8] {'hodlr'}, dimensions={0}, use_global_device_ids=true | all-gather | bytes 221184 | tf_op jit(solution)/shard_map/while/body/eval_jaxpr/all_gather | solution.py:83
  155.4 4.6 collective-permute-done
  166.2 13.7 %all_gather.9 = f32[8,3,2048]{2,1,0:T(4,128)S(1)} all-gather(f32[1,3,2048]{2,1,0:T(4,128)S(1)} %reshape.133), channel_id=1, replica_groups=mesh['slab'=32,'hodlr'=8] {'hodlr'}, dimensions={0}, use_global_device_ids=true | all-gather | bytes 221184 | tf_op jit(solution)/shard_map/while/body/eval_jaxpr/all_gather | solution.py:83
  185.0 4.6 collective-permute-done
  195.8 13.7 %all_gather.9 = f32[8,3,2048]{2,1,0:T(4,128)S(1)} all-gather(f32[1,3,2048]{2,1,0:T(4,128)S(1)} %reshape.133), channel_id=1, replica_groups=mesh['slab'=32,'hodlr'=8] {'hodlr'}, dimensions={0}, use_global_device_ids=true | all-gather | bytes 221184 | tf_op jit(solution)/shard_map/while/body/eval_jaxpr/all_gather | solution.py:83
  225.4 13.7 %all_gather.9 = f32[8,3,2048]{2,1,0:T(4,128)S(1)} all-gather(f32[1,3,2048]{2,1,0:T(4,128)S(1)} %reshape.133), channel_id=1, replica_groups=mesh['slab'=32,'hodlr'=8] {'hodlr'}, dimensions={0}, use_global_device_ids=true | all-gather | bytes 221184 | tf_op jit(solution)/shard_map/while/body/eval_jaxpr/all_gather | solution.py:83
  255.1 13.7 %all_gather.9 = f32[8,3,2048]{2,1,0:T(4,128)S(1)} all-gather(f32[1,3,2048]{2,1,0:T(4,128)S(1)} %reshape.133), channel_id=1, replica_groups=mesh['slab'=32,'hodlr'=8] {'hodlr'}, dimensions={0}, use_global_device_ids=true | all-gather | bytes 221184 | tf_op jit(solution)/shard_map/while/body/eval_jaxpr/all_gather | solution.py:83
  273.9 4.6 collective-permute-done
  284.7 13.7 %all_gather.9 = f32[8,3,2048]{2,1,0:T(4,128)S(1)} all-gather(f32[1,3,2048]{2,1,0:T(4,128)S(1)} %reshape.133), channel_id=1, replica_groups=mesh['slab'=32,'hodlr'=8] {'hodlr'}, dimensions={0}, use_global_device_ids=true | all-gather | bytes 221184 | tf_op jit(solution)/shard_map/while/body/eval_jaxpr/all_gather | solution.py:83
  303.6 4.6 collective-permute-done
  314.4 13.7 %all_gather.9 = f32[8,3,2048]{2,1,0:T(4,128)S(1)} all-gather(f32[1,3,2048]{2,1,0:T(4,128)S(1)} %reshape.133), channel_id=1, replica_groups=mesh['slab'=32,'hodlr'=8] {'hodlr'}, dimensions={0}, use_global_device_ids=true | all-gather | bytes 221184 | tf_op jit(solution)/shard_map/while/body/eval_jaxpr/all_gather | solution.py:83
  344.0 13.7 %all_gather.9 = f32[8,3,2048]{2,1,0:T(4,128)S(1)} all-gather(f32[1,3,2048]{2,1,0:T(4,128)S(1)} %reshape.133), channel_id=1, replica_groups=mesh['slab'=32,'hodlr'=8] {'hodlr'}, dimensions={0}, use_global_device_ids=true | all-gather | bytes 221184 | tf_op jit(solution)/shard_map/while/body/eval_jaxpr/all_gather | solution.py:83
  362.9 4.6 collective-permute-done
  373.7 13.7 %all_gather.9 = f32[8,3,2048]{2,1,0:T(4,128)S(1)} all-gather(f32[1,3,2048]{2,1,0:T(4,128)S(1)} %reshape.133), channel_id=1, replica_groups=mesh['slab'=32,'hodlr'=8] {'hodlr'}, dimensions={0}, use_global_device_ids=true | all-gather | bytes 221184 | tf_op jit(solution)/shard_map/while/body/eval_jaxpr/all_gather | solution.py:83
  392.5 4.6 collective-permute-done
  403.3 13.7 %all_gather.9 = f32[8,3,2048]{2,1,0:T(4,128)S(1)} all-gather(f32[1,3,2048]{2,1,0:T(4,128)S(1)} %reshape.133), channel_id=1, replica_groups=mesh['slab'=32,'hodlr'=8] {'hodlr'}, dimensions={0}, use_global_device_ids=true | all-gather | bytes 221184 | tf_op jit(solution)/shard_map/while/body/eval_jaxpr/all_gather | solution.py:83
  422.2 4.6 collective-permute-done
  432.9 13.7 %all_gather.9 = f32[8,3,2048]{2,1,0:T(4,128)S(1)} all-gather(f32[1,3,2048]{2,1,0:T(4,128)S(1)} %reshape.133), channel_id=1, replica_groups=mesh['slab'=32,'hodlr'=8] {'hodlr'}, dimensions={0}, use_global_device_ids=true | all-gather | bytes 221184 | tf_op jit(solution)/shard_map/while/body/eval_jaxpr/all_gather | solution.py:83
  462.6 13.7 %all_gather.9 = f32[8,3,2048]{2,1,0:T(4,128)S(1)} all-gather(f32[1,3,2048]{2,1,0:T(4,128)S(1)} %reshape.133), channel_id=1, replica_groups=mesh['slab'=32,'hodlr'=8] {'hodlr'}, dimensions={0}, use_global_device_ids=true | all-gather | bytes 221184 | tf_op jit(solution)/shard_map/while/body/eval_jaxpr/all_gather | solution.py:83
  481.4 4.6 collective-permute-done
  492.2 13.7 %all_gather.9 = f32[8,3,2048]{2,1,0:T(4,128)S(1)} all-gather(f32[1,3,2048]{2,1,0:T(4,128)S(1)} %reshape.133), channel_id=1, replica_groups=mesh['slab'=32,'hodlr'=8] {'hodlr'}, dimensions={0}, use_global_device_ids=true | all-gather | bytes 221184 | tf_op jit(solution)/shard_map/while/body/eval_jaxpr/all_gather | solution.py:83
  511.1 4.6 collective-permute-done
  521.9 13.7 %all_gather.9 = f32[8,3,2048]{2,1,0:T(4,128)S(1)} all-gather(f32[1,3,2048]{2,1,0:T(4,128)S(1)} %reshape.133), channel_id=1, replica_groups=mesh['slab'=32,'hodlr'=8] {'hodlr'}, dimensions={0}, use_global_device_ids=true | all-gather | bytes 221184 | tf_op jit(solution)/shard_map/while/body/eval_jaxpr/all_gather | solution.py:83
  540.7 4.6 collective-permute-done
  551.5 13.7 %all_gather.9 = f32[8,3,2048]{2,1,0:T(4,128)S(1)} all-gather(f32[1,3,2048]{2,1,0:T(4,128)S(1)} %reshape.133), channel_id=1, replica_groups=mesh['slab'=32,'hodlr'=8] {'hodlr'}, dimensions={0}, use_global_device_ids=true | all-gather | bytes 221184 | tf_op jit(solution)/shard_map/while/body/eval_jaxpr/all_gather | solution.py:83
  581.1 13.7 %all_gather.9 = f32[8,3,2048]{2,1,0:T(4,128)S(1)} all-gather(f32[1,3,2048]{2,1,0:T(4,128)S(1)} %reshape.133), channel_id=1, replica_groups=mesh['slab'=32,'hodlr'=8] {'hodlr'}, dimensions={0}, use_global_device_ids=true | all-gather | bytes 221184 | tf_op jit(solution)/shard_map/while/body/eval_jaxpr/all_gather | solution.py:83
  600.0 4.6 collective-permute-done
  610.8 13.7 %all_gather.9 = f32[8,3,2048]{2,1,0:T(4,128)S(1)} all-gather(f32[1,3,2048]{2,1,0:T(4,128)S(1)} %reshape.133), channel_id=1, replica_groups=mesh['slab'=32,'hodlr'=8] {'hodlr'}, dimensions={0}, use_global_device_ids=true | all-gather | bytes 221184 | tf_op jit(solution)/shard_map/while/body/eval_jaxpr/all_gather | solution.py:83
  629.6 4.6 collective-permute-done
  640.4 13.7 %all_gather.9 = f32[8,3,2048]{2,1,0:T(4,128)S(1)} all-gather(f32[1,3,2048]{2,1,0:T(4,128)S(1)} %reshape.133), channel_id=1, replica_groups=mesh['slab'=32,'hodlr'=8] {'hodlr'}, dimensions={0}, use_global_device_ids=true | all-gather | bytes 221184 | tf_op jit(solution)/shard_map/while/body/eval_jaxpr/all_gather | solution.py:83
  670.1 13.7 %all_gather.9 = f32[8,3,2048]{2,1,0:T(4,128)S(1)} all-gather(f32[1,3,2048]{2,1,0:T(4,128)S(1)} %reshape.133), channel_id=1, replica_groups=mesh['slab'=32,'hodlr'=8] {'hodlr'}, dimensions={0}, use_global_device_ids=true | all-gather | bytes 221184 | tf_op jit(solution)/shard_map/while/body/eval_jaxpr/all_gather | solution.py:83
  699.7 13.7 %all_gather.9 = f32[8,3,2048]{2,1,0:T(4,128)S(1)} all-gather(f32[1,3,2048]{2,1,0:T(4,128)S(1)} %reshape.133), channel_id=1, replica_groups=mesh['slab'=32,'hodlr'=8] {'hodlr'}, dimensions={0}, use_global_device_ids=true | all-gather | bytes 221184 | tf_op jit(solution)/shard_map/while/body/eval_jaxpr/all_gather | solution.py:83
  729.4 13.7 %all_gather.9 = f32[8,3,2048]{2,1,0:T(4,128)S(1)} all-gather(f32[1,3,2048]{2,1,0:T(4,128)S(1)} %reshape.133), channel_id=1, replica_groups=mesh['slab'=32,'hodlr'=8] {'hodlr'}, dimensions={0}, use_global_device_ids=true | all-gather | bytes 221184 | tf_op jit(solution)/shard_map/while/body/eval_jaxpr/all_gather | solution.py:83
  759.0 13.7 %all_gather.9 = f32[8,3,2048]{2,1,0:T(4,128)S(1)} all-gather(f32[1,3,2048]{2,1,0:T(4,128)S(1)} %reshape.133), channel_id=1, replica_groups=mesh['slab'=32,'hodlr'=8] {'hodlr'}, dimensions={0}, use_global_device_ids=true | all-gather | bytes 221184 | tf_op jit(solution)/shard_map/while/body/eval_jaxpr/all_gather | solution.py:83
  788.6 13.7 %all_gather.9 = f32[8,3,2048]{2,1,0:T(4,128)S(1)} all-gather(f32[1,3,2048]{2,1,0:T(4,128)S(1)} %reshape.133), channel_id=1, replica_groups=mesh['slab'=32,'hodlr'=8] {'hodlr'}, dimensions={0}, use_global_device_ids=true | all-gather | bytes 221184 | tf_op jit(solution)/shard_map/while/body/eval_jaxpr/all_gather | solution.py:83
  818.3 13.7 %all_gather.9 = f32[8,3,2048]{2,1,0:T(4,128)S(1)} all-gather(f32[1,3,2048]{2,1,0:T(4,128)S(1)} %reshape.133), channel_id=1, replica_groups=mesh['slab'=32,'hodlr'=8] {'hodlr'}, dimensions={0}, use_global_device_ids=true | all-gather | bytes 221184 | tf_op jit(solution)/shard_map/while/body/eval_jaxpr/all_gather | solution.py:83
  847.9 13.7 %all_gather.9 = f32[8,3,2048]{2,1,0:T(4,128)S(1)} all-gather(f32[1,3,2048]{2,1,0:T(4,128)S(1)} %reshape.133), channel_id=1, replica_groups=mesh['slab'=32,'hodlr'=8] {'hodlr'}, dimensions={0}, use_global_device_ids=true | all-gather | bytes 221184 | tf_op jit(solution)/shard_map/while/body/eval_jaxpr/all_gather | solution.py:83
  877.6 13.7 %all_gather.9 = f32[8,3,2048]{2,1,0:T(4,128)S(1)} all-gather(f32[1,3,2048]{2,1,0:T(4,128)S(1)} %reshape.133), channel_id=1, replica_groups=mesh['slab'=32,'hodlr'=8] {'hodlr'}, dimensions={0}, use_global_device_ids=true | all-gather | bytes 221184 | tf_op jit(solution)/shard_map/while/body/eval_jaxpr/all_gather | solution.py:83
  907.2 13.7 %all_gather.9 = f32[8,3,2048]{2,1,0:T(4,128)S(1)} all-gather(f32[1,3,2048]{2,1,0:T(4,128)S(1)} %reshape.133), channel_id=1, replica_groups=mesh['slab'=32,'hodlr'=8] {'hodlr'}, dimensions={0}, use_global_device_ids=true | all-gather | bytes 221184 | tf_op jit(solution)/shard_map/while/body/eval_jaxpr/all_gather | solution.py:83
  936.9 13.7 %all_gather.9 = f32[8,3,2048]{2,1,0:T(4,128)S(1)} all-gather(f32[1,3,2048]{2,1,0:T(4,128)S(1)} %reshape.133), channel_id=1, replica_groups=mesh['slab'=32,'hodlr'=8] {'hodlr'}, dimensions={0}, use_global_device_ids=true | all-gather | bytes 221184 | tf_op jit(solution)/shard_map/while/body/eval_jaxpr/all_gather | solution.py:83
  (664 shorter events, 439.2 us)
Async XLA Ops:
  0.1 10.9 %collective-permute-start = (bf16[32,2048]{1,0:T(8,128)(2,1)S(1)}, bf16[32,2048]{1,0:T(8,128)(2,1)S(1)}, u32[]{:S(2)}, u32[]{:S(2)}) collective-permute-start(bf16[32,2048]{1,0:T(8,128)(2,1)S(1)} %broadcast_select_fusion.2), channel_id=1, source_target_pairs={{0,8},{8,16},{16,24},{24,32},{32,40},{40,48},{48,56},{56,64},{64,7... | collective-permute-start | bytes 393224 | tf_op jit(solution)/shard_map/while/body/eval_jaxpr/ppermute | solution.py:10
  12.0 20.2 %copy-start = (bf16[4,64,2048]{2,1,0:T(8,128)(2,1)S(1)}, bf16[4,64,2048]{2,1,0:T(8,128)(2,1)}, u32[]{:S(2)}) copy-start(bf16[4,64,2048]{2,1,0:T(8,128)(2,1)} %get-tuple-element.299) | copy-start | bytes 3145732 | tf_op jit(solution)/shard_map/while
  32.5 8.9 collective-permute-start
  42.4 19.5 %copy-start = (bf16[4,64,2048]{2,1,0:T(8,128)(2,1)S(1)}, bf16[4,64,2048]{2,1,0:T(8,128)(2,1)}, u32[]{:S(2)}) copy-start(bf16[4,64,2048]{2,1,0:T(8,128)(2,1)} %get-tuple-element.299) | copy-start | bytes 3145732 | tf_op jit(solution)/shard_map/while
  62.2 8.9 collective-permute-start
  72.0 19.5 %copy-start = (bf16[4,64,2048]{2,1,0:T(8,128)(2,1)S(1)}, bf16[4,64,2048]{2,1,0:T(8,128)(2,1)}, u32[]{:S(2)}) copy-start(bf16[4,64,2048]{2,1,0:T(8,128)(2,1)} %get-tuple-element.299) | copy-start | bytes 3145732 | tf_op jit(solution)/shard_map/while
  91.8 8.9 collective-permute-start
  101.7 19.5 %copy-start = (bf16[4,64,2048]{2,1,0:T(8,128)(2,1)S(1)}, bf16[4,64,2048]{2,1,0:T(8,128)(2,1)}, u32[]{:S(2)}) copy-start(bf16[4,64,2048]{2,1,0:T(8,128)(2,1)} %get-tuple-element.299) | copy-start | bytes 3145732 | tf_op jit(solution)/shard_map/while
  121.5 8.9 collective-permute-start
  131.3 19.5 %copy-start = (bf16[4,64,2048]{2,1,0:T(8,128)(2,1)S(1)}, bf16[4,64,2048]{2,1,0:T(8,128)(2,1)}, u32[]{:S(2)}) copy-start(bf16[4,64,2048]{2,1,0:T(8,128)(2,1)} %get-tuple-element.299) | copy-start | bytes 3145732 | tf_op jit(solution)/shard_map/while
  151.1 8.9 collective-permute-start
  160.9 19.5 %copy-start = (bf16[4,64,2048]{2,1,0:T(8,128)(2,1)S(1)}, bf16[4,64,2048]{2,1,0:T(8,128)(2,1)}, u32[]{:S(2)}) copy-start(bf16[4,64,2048]{2,1,0:T(8,128)(2,1)} %get-tuple-element.299) | copy-start | bytes 3145732 | tf_op jit(solution)/shard_map/while
  180.8 8.9 collective-permute-start
  190.6 19.5 %copy-start = (bf16[4,64,2048]{2,1,0:T(8,128)(2,1)S(1)}, bf16[4,64,2048]{2,1,0:T(8,128)(2,1)}, u32[]{:S(2)}) copy-start(bf16[4,64,2048]{2,1,0:T(8,128)(2,1)} %get-tuple-element.299) | copy-start | bytes 3145732 | tf_op jit(solution)/shard_map/while
  210.4 8.9 collective-permute-start
  220.2 19.5 %copy-start = (bf16[4,64,2048]{2,1,0:T(8,128)(2,1)S(1)}, bf16[4,64,2048]{2,1,0:T(8,128)(2,1)}, u32[]{:S(2)}) copy-start(bf16[4,64,2048]{2,1,0:T(8,128)(2,1)} %get-tuple-element.299) | copy-start | bytes 3145732 | tf_op jit(solution)/shard_map/while
  240.0 8.9 collective-permute-start
  269.7 8.9 collective-permute-start
  299.3 8.9 collective-permute-start
  309.2 19.5 %copy-start = (bf16[4,64,2048]{2,1,0:T(8,128)(2,1)S(1)}, bf16[4,64,2048]{2,1,0:T(8,128)(2,1)}, u32[]{:S(2)}) copy-start(bf16[4,64,2048]{2,1,0:T(8,128)(2,1)} %get-tuple-element.299) | copy-start | bytes 3145732 | tf_op jit(solution)/shard_map/while
  329.0 8.9 collective-permute-start
  358.6 8.9 collective-permute-start
  388.3 8.9 collective-permute-start
  417.9 8.9 collective-permute-start
  427.7 19.5 %copy-start = (bf16[4,64,2048]{2,1,0:T(8,128)(2,1)S(1)}, bf16[4,64,2048]{2,1,0:T(8,128)(2,1)}, u32[]{:S(2)}) copy-start(bf16[4,64,2048]{2,1,0:T(8,128)(2,1)} %get-tuple-element.299) | copy-start | bytes 3145732 | tf_op jit(solution)/shard_map/while
  447.5 8.9 collective-permute-start
  477.2 8.9 collective-permute-start
  506.8 8.9 collective-permute-start
  516.6 19.5 %copy-start = (bf16[4,64,2048]{2,1,0:T(8,128)(2,1)S(1)}, bf16[4,64,2048]{2,1,0:T(8,128)(2,1)}, u32[]{:S(2)}) copy-start(bf16[4,64,2048]{2,1,0:T(8,128)(2,1)} %get-tuple-element.299) | copy-start | bytes 3145732 | tf_op jit(solution)/shard_map/while
  536.5 8.9 collective-permute-start
  546.3 19.5 %copy-start = (bf16[4,64,2048]{2,1,0:T(8,128)(2,1)S(1)}, bf16[4,64,2048]{2,1,0:T(8,128)(2,1)}, u32[]{:S(2)}) copy-start(bf16[4,64,2048]{2,1,0:T(8,128)(2,1)} %get-tuple-element.299) | copy-start | bytes 3145732 | tf_op jit(solution)/shard_map/while
  566.1 8.9 collective-permute-start
  595.7 8.9 collective-permute-start
  625.4 8.9 collective-permute-start
  635.2 19.5 %copy-start = (bf16[4,64,2048]{2,1,0:T(8,128)(2,1)S(1)}, bf16[4,64,2048]{2,1,0:T(8,128)(2,1)}, u32[]{:S(2)}) copy-start(bf16[4,64,2048]{2,1,0:T(8,128)(2,1)} %get-tuple-element.299) | copy-start | bytes 3145732 | tf_op jit(solution)/shard_map/while
  655.0 8.9 collective-permute-start
  664.9 19.5 %copy-start = (bf16[4,64,2048]{2,1,0:T(8,128)(2,1)S(1)}, bf16[4,64,2048]{2,1,0:T(8,128)(2,1)}, u32[]{:S(2)}) copy-start(bf16[4,64,2048]{2,1,0:T(8,128)(2,1)} %get-tuple-element.299) | copy-start | bytes 3145732 | tf_op jit(solution)/shard_map/while
  684.7 8.9 collective-permute-start
  714.3 8.9 collective-permute-start
  744.0 8.9 collective-permute-start
  753.8 19.5 %copy-start = (bf16[4,64,2048]{2,1,0:T(8,128)(2,1)S(1)}, bf16[4,64,2048]{2,1,0:T(8,128)(2,1)}, u32[]{:S(2)}) copy-start(bf16[4,64,2048]{2,1,0:T(8,128)(2,1)} %get-tuple-element.299) | copy-start | bytes 3145732 | tf_op jit(solution)/shard_map/while
  773.6 8.9 collective-permute-start
  803.2 8.9 collective-permute-start
  832.9 8.9 collective-permute-start
  862.5 8.9 collective-permute-start
  872.4 19.5 %copy-start = (bf16[4,64,2048]{2,1,0:T(8,128)(2,1)S(1)}, bf16[4,64,2048]{2,1,0:T(8,128)(2,1)}, u32[]{:S(2)}) copy-start(bf16[4,64,2048]{2,1,0:T(8,128)(2,1)} %get-tuple-element.299) | copy-start | bytes 3145732 | tf_op jit(solution)/shard_map/while
  892.2 8.9 collective-permute-start
  921.8 8.9 collective-permute-start
  (17 other events, 312.0 us)
where the time goes:
time: 958 us; the launch traced here: 952 us
  blocking collectives  439 us (46%)
  matrix products  185 us (19%)
  waiting for transfers between devices  149 us (16%)
  local copies, waits for them, and re-layouts  81.8 us (9%)
  starting transfers between devices  63.1 us (7%)
  other arithmetic  30.5 us (3%)
    all_gather x32, blocking collectives, apply(): gathered = lax.all_gather(partial_value[None], 'hodlr', axis=0, tiled=True)  439 us
    ppermute x32, waiting for transfers between devices, passed_along(): return lax.ppermute(block, axis, route)  149 us
    dot_general x32, matrix products, local_part(): jnp.einsum('sbj,bjo->sbo', w.reshape(rows, nleaf, leaf_size), leaf, prefe...  97 us
    ppermute x32, starting transfers between devices, passed_along(): return lax.ppermute(block, axis, route)  63.1 us
    dot_general x32, matrix products, partials_of(): jnp.einsum('sn,crn->csr', w, factors, preferred_element_type=jnp.float32)  52.1 us
    slice x32, local copies, waits for them, and re-layouts, local_part(): right[3].reshape(rank, block_list, block_size)  31.1 us
    slice x32, local copies, waits for them, and re-layouts, local_part(): left[3].reshape(rank, block_list, block_size)  31.1 us
    convert_element_type x32, other arithmetic, advance(): (source.astype(jnp.float32) + incoming.astype(jnp.float32)).astype(jnp.bf...  30 us
  transfers between devices with their start and end apart: 32, of which 32 were waited for; matrix products, arithmetic and copies ran while one was open for 8% of the time, Pallas kernels for 0%

commit v1 on v0

v1 whole, which is shorter than its diff:
```python
import functools

import jax
import jax.numpy as jnp
from jax import lax
from jax.experimental import pallas as pl
from jax.experimental.pallas import tpu as pltpu
from jax.sharding import PartitionSpec as P

MESH = pl.DeviceIdType.MESH
GROUPS = 4
WHOLE_SLABS = 5
PEERS = 8


def flipped(member, j):
    bits = (lax.rem(member, 2), lax.rem(lax.div(member, 2), 2), lax.div(member, 4))
    total = 0
    for i, bit in enumerate(bits):
        total = total + (1 << i) * ((1 - bit) if (j >> i) & 1 else bit)
    return total


def kernel(
    slabs, whole, src, leaf, v, u, out,
    u_prev, w_buf, l_in, p_in, p_self, l_send, l_wide, p_send, back, back_in,
    u_ss, u_rs, l_ss, l_rs, p_ss, p_rs, q_ss, q_rs, b_ss, b_rs,
):
    k = lax.axis_index("slab")
    m = lax.axis_index("hodlr")
    groups, rows, width = src.shape
    nleaf, size = leaf.shape[0], leaf.shape[1]

    first, last = k == 0, k == slabs - 1
    whole_send = k + 1 < whole
    split_send = jnp.logical_and(k + 1 >= whole, k < slabs - 1)
    whole_recv = jnp.logical_and(k >= 1, k < whole)
    split_recv = k >= whole
    own = jnp.logical_or(whole_send, last)

    def remote(source, target, send, recv, slab, member):
        return pltpu.make_async_remote_copy(
            src_ref=source, dst_ref=target, send_sem=send, recv_sem=recv,
            device_id=(slab, member), device_id_type=MESH,
        )

    def u_copy():
        return remote(u, u_prev, u_ss, u_rs, k + 1, m)

    def l_copy(g):
        return remote(l_send.at[g], l_in.at[g], l_ss.at[g], l_rs.at[g], k + 1, m)

    def back_copy(g):
        return remote(back.at[g], back_in.at[g], b_ss.at[g], b_rs.at[g], k - 1, m)

    def tile_of(j):
        return 1 if j == 1 else 0

    def p_copy(g, j):
        if j == 0:
            return remote(
                p_send.at[g, pl.ds(2, 2)], p_in.at[g, pl.ds(0, 2)], p_ss.at[g, 0], p_rs.at[g, 0], k + 1, m
            )
        return remote(
            p_send.at[g, tile_of(j)], p_in.at[g, j + 1], p_ss.at[g, j], p_rs.at[g, j], k + 1, flipped(m, j)
        )

    def q_copy(g, j):
        return remote(
            p_send.at[g, tile_of(j)], p_self.at[g, j], q_ss.at[g, j], q_rs.at[g, j], k, flipped(m, j)
        )

    barrier = pltpu.get_barrier_semaphore()

    def greet(slab, member):
        pl.semaphore_signal(barrier, inc=1, device_id=(slab, member), device_id_type=MESH)

    for j in range(1, PEERS):
        greet(k, flipped(m, j))

    @pl.when(k > 0)
    def _():
        for j in range(PEERS):
            greet(k - 1, flipped(m, j))

    @pl.when(k < slabs - 1)
    def _():
        for j in range(PEERS):
            greet(k + 1, flipped(m, j))

    edge = jnp.logical_or(first, last)

    @pl.when(edge)
    def _():
        pl.semaphore_wait(barrier, 2 * PEERS - 1)

    @pl.when(jnp.logical_not(edge))
    def _():
        pl.semaphore_wait(barrier, 3 * PEERS - 1)

    @pl.when(split_send)
    def _():
        u_copy().start()

    low = lax.broadcasted_iota(jnp.int32, (rows, 128), 1) < 64

    def low_rank(read, four_left, four_right, factors):
        one = read(4) + read(5) + read(6) + read(7)
        two = read(2) + read(3)
        three = read(1)
        top = jnp.where(low, one, two)
        left = jnp.concatenate([top, jnp.where(low, three, four_left)], axis=1).astype(jnp.bfloat16)
        right = jnp.concatenate([top, jnp.where(low, three, four_right)], axis=1).astype(jnp.bfloat16)
        return (
            jnp.dot(left, factors[:, :size], preferred_element_type=jnp.float32),
            jnp.dot(right, factors[:, size:], preferred_element_type=jnp.float32),
        )

    @pl.when(split_recv)
    def _():
        u_copy().wait_recv()

    @pl.loop(0, groups)
    def _(g):
        @pl.when(first)
        def _():
            w_buf[...] = src[g]

        @pl.when(whole_recv)
        def _():
            l_copy(g).wait_recv()
            w_buf[...] = (src[g].astype(jnp.float32) + l_in[g].astype(jnp.float32)).astype(jnp.bfloat16)

        @pl.when(split_recv)
        def _():
            for j in range(PEERS):
                p_copy(g, j).wait_recv()
            parts = low_rank(
                lambda j: p_in[g, j + 1].astype(jnp.float32),
                p_in[g, 0].astype(jnp.float32), p_in[g, 1].astype(jnp.float32), u_prev,
            )
            l_copy(g).wait_recv()
            for i, part in enumerate(parts):
                cols = slice(i * size, (i + 1) * size)
                front = (l_in[g, :, cols].astype(jnp.float32) + part).astype(jnp.bfloat16)
                back[g, :, cols] = front
                w_buf[:, cols] = (
                    src[g, :, cols].astype(jnp.float32) + front.astype(jnp.float32)
                ).astype(jnp.bfloat16)

        halves = [
            lax.dot_general(
                w_buf[:, i * size : (i + 1) * size], v[:, i * size : (i + 1) * size],
                (((1,), (1,)), ((), ())), preferred_element_type=jnp.float32,
            )
            for i in range(2)
        ]
        total = halves[0] + halves[1]
        p_send[g, 0] = total[:, :128].astype(jnp.bfloat16)
        p_send[g, 1] = total[:, 128:].astype(jnp.bfloat16)
        p_send[g, 2] = halves[1][:, 128:].astype(jnp.bfloat16)
        p_send[g, 3] = halves[0][:, 128:].astype(jnp.bfloat16)

        @pl.when(split_send)
        def _():
            for j in (6, 7, 4, 5, 2, 3, 1, 0):
                p_copy(g, j).start()

        @pl.when(own)
        def _():
            for j in (6, 7, 4, 5, 2, 3, 1):
                q_copy(g, j).start()

        for i in range(nleaf):
            cols = slice(i * size, (i + 1) * size)
            part = jnp.dot(w_buf[:, cols], leaf[i], preferred_element_type=jnp.float32)
            l_wide[g, :, cols] = part
            l_send[g, :, cols] = part.astype(jnp.bfloat16)

        @pl.when(split_send)
        def _():
            l_copy(g).start()

        @pl.when(split_recv)
        def _():
            back_copy(g).start()

    @pl.when(own)
    def _():
        @pl.loop(0, groups)
        def _(g):
            for j in range(1, PEERS):
                q_copy(g, j).wait_recv()
            parts = low_rank(
                lambda j: p_self[g, j].astype(jnp.float32),
                p_send[g, 2].astype(jnp.float32), p_send[g, 3].astype(jnp.float32), u,
            )
            for i, part in enumerate(parts):
                cols = slice(i * size, (i + 1) * size)
                front = (l_wide[g, :, cols] + part).astype(jnp.bfloat16)
                out[g, :, cols] = front
                l_send[g, :, cols] = front

            @pl.when(whole_send)
            def _():
                l_copy(g).start()

        @pl.loop(0, groups)
        def _(g):
            for j in range(1, PEERS):
                q_copy(g, j).wait_send()

            @pl.when(whole_send)
            def _():
                l_copy(g).wait_send()

    @pl.when(split_send)
    def _():
        u_copy().wait_send()

        @pl.loop(0, groups)
        def _(g):
            l_copy(g).wait_send()
            for j in range(PEERS):
                p_copy(g, j).wait_send()
            back_copy(g).wait_recv()
            out[g] = back_in[g]

    @pl.when(split_recv)
    def _():
        @pl.loop(0, groups)
        def _(g):
            back_copy(g).wait_send()


def solution(mesh, groups=GROUPS, whole=WHOLE_SLABS):
    slabs = mesh.shape["slab"]

    def local(sources, leaves, v_rows, u_rows):
        shots, width = sources.shape[1:]
        levels, rank = v_rows.shape[1:3]
        rows = shots // groups
        bf16, wide = jnp.bfloat16, jnp.float32
        dma = pltpu.SemaphoreType.DMA
        vmem = pl.BlockSpec(memory_space=pltpu.VMEM)
        swept = pl.pallas_call(
            functools.partial(kernel, slabs, whole),
            out_shape=jax.ShapeDtypeStruct((groups, rows, width), bf16),
            in_specs=[vmem] * 4,
            out_specs=vmem,
            scratch_shapes=[
                pltpu.VMEM((levels * rank, width), bf16),
                pltpu.VMEM((rows, width), bf16),
                pltpu.VMEM((groups, rows, width), bf16),
                pltpu.VMEM((groups, 9, rows, 128), bf16),
                pltpu.VMEM((groups, PEERS, rows, 128), bf16),
                pltpu.VMEM((groups, rows, width), bf16),
                pltpu.VMEM((groups, rows, width), wide),
                pltpu.VMEM((groups, 4, rows, 128), bf16),
                pltpu.VMEM((groups, rows, width), bf16),
                pltpu.VMEM((groups, rows, width), bf16),
                dma, dma,
                dma((groups,)), dma((groups,)),
                dma((groups, PEERS)), dma((groups, PEERS)),
                dma((groups, PEERS)), dma((groups, PEERS)),
                dma((groups,)), dma((groups,)),
            ],
            compiler_params=pltpu.CompilerParams(collective_id=0, has_side_effects=True),
            name="sweep",
        )(
            sources[0].reshape(groups, rows, width),
            leaves[0],
            v_rows[0].reshape(levels * rank, width),
            u_rows[0].reshape(levels * rank, width),
        )
        return swept.reshape(1, shots, width)

    return jax.shard_map(
        local,
        mesh=mesh,
        in_specs=(
            P("slab", None, "hodlr"),
            P("slab", "hodlr", None, None),
            P("slab", None, None, "hodlr"),
            P("slab", None, None, "hodlr"),
        ),
        out_specs=P("slab", None, "hodlr"),
        check_vma=False,
    )
```

time: 958 us -> 171 us (0.18)
  the two profiles are of different devices: /device:TPU:7 before, /device:TPU:231 now
where the time goes in v1:
time: 171 us
  Pallas kernels  169 us (99%)
    pallas_call x1, Pallas kernels, local(): pl.pallas_call(functools.partial(kernel, slabs, whole), out_shape=jax.Sha...  169 us

profile of v1, /device:TPU:231, one launch (start us, length us, event | category | flops | bytes accessed | tf_op | source)
XLA Modules:
  0.0 170.5 jit_solution(9536369557377156619)
XLA Ops:
  0.0 169.0 %sweep.1 = bf16[4,8,2048]{2,1,0:T(8,128)(2,1)} custom-call(bf16[4,8,2048]{2,1,0:T(8,128)(2,1)} %bitcast.9, bf16[2,1024,1024]{2,1,0:T(8,128)(2,1)} %bitcast.5, bf16[256,2048]{1,0:T(8,128)(2,1)} %bitcast.6, bf16[256,2048]{1,0:T(8,128)(2,1)} %bitcast.7), custom_call_target="tpu_custom_call" | custom-call | tf_op jit(solution)/shard_map/sweep/pallas_call | solution.py:246
  169.0 1.6 copy.6

commit v2 on v1

v2 whole, which is shorter than its diff:
```python
import functools

import jax
import jax.numpy as jnp
from jax import lax
from jax.experimental import pallas as pl
from jax.experimental.pallas import tpu as pltpu
from jax.sharding import PartitionSpec as P

MESH = pl.DeviceIdType.MESH
GROUPS = 4
WHOLE_SLABS = 4
PEERS = 8


def flipped(member, j):
    bits = (lax.rem(member, 2), lax.rem(lax.div(member, 2), 2), lax.div(member, 4))
    total = 0
    for i, bit in enumerate(bits):
        total = total + (1 << i) * ((1 - bit) if (j >> i) & 1 else bit)
    return total


def kernel(
    slabs, whole, src_hbm, leaf_hbm, v_hbm, u_hbm, out,
    src, leaf, v, u, load_sem, u_prev, w_buf, l_in, p_in, p_self, l_send, l_wide, p_send, back, back_in,
    u_ss, u_rs, l_ss, l_rs, p_ss, p_rs, q_ss, q_rs, b_ss, b_rs,
):
    k = lax.axis_index("slab")
    m = lax.axis_index("hodlr")
    groups, rows, width = src.shape
    nleaf, size = leaf.shape[0], leaf.shape[1]
    cross = u_prev.shape[0]
    bf16, wide = jnp.bfloat16, jnp.float32

    first, last = k == 0, k == slabs - 1
    whole_send = k + 1 < whole
    split_send = jnp.logical_and(k + 1 >= whole, k < slabs - 1)
    whole_recv = jnp.logical_and(k >= 1, k < whole)
    split_recv = k >= whole
    own = jnp.logical_or(whole_send, last)
    halves = [slice(i * size, (i + 1) * size) for i in range(nleaf)]

    def remote(source, target, send, recv, slab, member):
        return pltpu.make_async_remote_copy(
            src_ref=source, dst_ref=target, send_sem=send, recv_sem=recv,
            device_id=(slab, member), device_id_type=MESH,
        )

    def u_copy():
        return remote(u_hbm.at[pl.ds(0, cross)], u_prev, u_ss, u_rs, k + 1, m)

    def l_copy(g, i):
        return remote(l_send.at[g, i], l_in.at[g, i], l_ss.at[g, i], l_rs.at[g, i], k + 1, m)

    def back_copy(g):
        return remote(back.at[g], back_in.at[g], b_ss.at[g], b_rs.at[g], k - 1, m)

    def tile_of(j):
        return 1 if j == 1 else 0

    def p_copy(g, j):
        return remote(
            p_send.at[g, tile_of(j)], p_in.at[g, j], p_ss.at[g, j], p_rs.at[g, j], k + 1, flipped(m, j)
        )

    def q_copy(g, j):
        return remote(
            p_send.at[g, tile_of(j)], p_self.at[g, j], q_ss.at[g, j], q_rs.at[g, j], k, flipped(m, j)
        )

    loads = [
        pltpu.make_async_copy(source, target, load_sem.at[i])
        for i, (source, target) in enumerate(((src_hbm, src), (v_hbm, v), (leaf_hbm, leaf), (u_hbm, u)))
    ]
    for load in loads:
        load.start()

    barrier = pltpu.get_barrier_semaphore()

    def greet(slab, member):
        pl.semaphore_signal(barrier, inc=1, device_id=(slab, member), device_id_type=MESH)

    for j in range(1, PEERS):
        greet(k, flipped(m, j))

    @pl.when(k > 0)
    def _():
        for j in range(PEERS):
            greet(k - 1, flipped(m, j))

    @pl.when(k < slabs - 1)
    def _():
        for j in range(PEERS):
            greet(k + 1, flipped(m, j))

    edge = jnp.logical_or(first, last)

    @pl.when(edge)
    def _():
        pl.semaphore_wait(barrier, 2 * PEERS - 1)

    @pl.when(jnp.logical_not(edge))
    def _():
        pl.semaphore_wait(barrier, 3 * PEERS - 1)

    @pl.when(split_send)
    def _():
        u_copy().start()

    low = lax.broadcasted_iota(jnp.int32, (rows, 128), 1) < 64

    def low_rank(read, factors):
        one = read(4) + read(5) + read(6) + read(7)
        two = read(2) + read(3)
        top = jnp.where(low, one, two)
        both = jnp.concatenate([top, read(1)], axis=1).astype(bf16)[:, :cross]
        return [jnp.dot(both, factors[:cross, cols], preferred_element_type=wide) for cols in halves]

    for load in loads[:2]:
        load.wait()

    @pl.when(jnp.logical_not(first))
    def _():
        for load in loads[2:]:
            load.wait()

    @pl.when(split_recv)
    def _():
        u_copy().wait_recv()

    @pl.loop(0, groups)
    def _(g):
        @pl.when(first)
        def _():
            for i, cols in enumerate(halves):
                w_buf[g, i] = src[g, :, cols]

        @pl.when(whole_recv)
        def _():
            for i, cols in enumerate(halves):
                l_copy(g, i).wait_recv()
                w_buf[g, i] = (src[g, :, cols].astype(wide) + l_in[g, i].astype(wide)).astype(bf16)

        @pl.when(split_recv)
        def _():
            for j in range(1, PEERS):
                p_copy(g, j).wait_recv()
            parts = low_rank(lambda j: p_in[g, j].astype(wide), u_prev)
            for i, cols in enumerate(halves):
                l_copy(g, i).wait_recv()
                front = (l_in[g, i].astype(wide) + parts[i]).astype(bf16)
                back[g, i] = front
                w_buf[g, i] = (src[g, :, cols].astype(wide) + front.astype(wide)).astype(bf16)

        inner = [
            lax.dot_general(w_buf[g, i], v[:, cols], (((1,), (1,)), ((), ())), preferred_element_type=wide)
            for i, cols in enumerate(halves)
        ]
        total = inner[0] + inner[1]
        p_send[g, 0] = total[:, :128].astype(bf16)
        p_send[g, 1] = total[:, 128:].astype(bf16)
        for i in range(nleaf):
            p_send[g, 2 + i] = jnp.where(low, 0.0, inner[1 - i][:, 128:]).astype(bf16)

        @pl.when(split_send)
        def _():
            for j in (4, 6, 5, 7, 2, 3, 1):
                p_copy(g, j).start()

        @pl.when(own)
        def _():
            for j in (4, 6, 5, 7, 2, 3, 1):
                q_copy(g, j).start()

        @pl.when(split_send)
        def _():
            for i, cols in enumerate(halves):
                part = jnp.dot(w_buf[g, i], leaf[i], preferred_element_type=wide)
                part += jnp.dot(p_send[g, 2 + i], u[cross - 64 :, cols], preferred_element_type=wide)
                l_send[g, i] = part.astype(bf16)
                l_copy(g, i).start()

        @pl.when(split_recv)
        def _():
            back_copy(g).start()

    @pl.when(first)
    def _():
        for load in loads[2:]:
            load.wait()

    def stacked(array):
        return array.astype(wide).reshape(groups * rows, array.shape[-1]).astype(bf16)

    @pl.when(own)
    def _():
        for i, cols in enumerate(halves):
            part = jnp.dot(stacked(w_buf[:, i]), leaf[i], preferred_element_type=wide)
            part += jnp.dot(stacked(p_send[:, 2 + i]), u[cross - 64 :, cols], preferred_element_type=wide)
            l_wide[:, i] = part.reshape(groups, rows, size)

        @pl.loop(0, groups)
        def _(g):
            for j in range(1, PEERS):
                q_copy(g, j).wait_recv()
            parts = low_rank(lambda j: p_self[g, j].astype(wide), u)
            for i, cols in enumerate(halves):
                front = (l_wide[g, i] + parts[i]).astype(bf16)
                out[g, :, cols] = front
                l_send[g, i] = front

                @pl.when(whole_send)
                def _(i=i):
                    l_copy(g, i).start()

        @pl.loop(0, groups)
        def _(g):
            for j in range(1, PEERS):
                q_copy(g, j).wait_send()

            @pl.when(whole_send)
            def _():
                for i in range(nleaf):
                    l_copy(g, i).wait_send()

    @pl.when(split_send)
    def _():
        u_copy().wait_send()

        @pl.loop(0, groups)
        def _(g):
            for i in range(nleaf):
                l_copy(g, i).wait_send()
            for j in range(1, PEERS):
                p_copy(g, j).wait_send()
            back_copy(g).wait_recv()
            for i, cols in enumerate(halves):
                out[g, :, cols] = back_in[g, i]

    @pl.when(split_recv)
    def _():
        @pl.loop(0, groups)
        def _(g):
            back_copy(g).wait_send()


def solution(mesh, groups=GROUPS, whole=WHOLE_SLABS):
    slabs = mesh.shape["slab"]

    def local(sources, leaves, v_rows, u_rows):
        shots, width = sources.shape[1:]
        nleaf, size = leaves.shape[1:3]
        levels, rank = v_rows.shape[1:3]
        rows = shots // groups
        bf16, wide = jnp.bfloat16, jnp.float32
        dma = pltpu.SemaphoreType.DMA
        vmem = pl.BlockSpec(memory_space=pltpu.VMEM)

        def split(dtype):
            return pltpu.VMEM((groups, nleaf, rows, size), dtype)

        swept = pl.pallas_call(
            functools.partial(kernel, slabs, whole),
            out_shape=jax.ShapeDtypeStruct((groups, rows, width), bf16),
            in_specs=[pl.BlockSpec(memory_space=pl.ANY)] * 4,
            out_specs=vmem,
            scratch_shapes=[
                pltpu.VMEM((groups, rows, width), bf16),
                pltpu.VMEM((nleaf, size, size), bf16),
                pltpu.VMEM((levels * rank, width), bf16),
                pltpu.VMEM((levels * rank, width), bf16),
                dma((4,)),
                pltpu.VMEM(((levels - 1) * rank, width), bf16),
                split(bf16),
                split(bf16),
                pltpu.VMEM((groups, PEERS, rows, 128), bf16),
                pltpu.VMEM((groups, PEERS, rows, 128), bf16),
                split(bf16),
                split(wide),
                pltpu.VMEM((groups, 2 + nleaf, rows, 128), bf16),
                split(bf16),
                split(bf16),
                dma, dma,
                dma((groups, nleaf)), dma((groups, nleaf)),
                dma((groups, PEERS)), dma((groups, PEERS)),
                dma((groups, PEERS)), dma((groups, PEERS)),
                dma((groups,)), dma((groups,)),
            ],
            compiler_params=pltpu.CompilerParams(collective_id=0, has_side_effects=True),
            name="sweep",
        )(
            sources[0].reshape(groups, rows, width),
            leaves[0],
            v_rows[0].reshape(levels * rank, width),
            u_rows[0].reshape(levels * rank, width),
        )
        return swept.reshape(1, shots, width)

    return jax.shard_map(
        local,
        mesh=mesh,
        in_specs=(
            P("slab", None, "hodlr"),
            P("slab", "hodlr", None, None),
            P("slab", None, None, "hodlr"),
            P("slab", None, None, "hodlr"),
        ),
        out_specs=P("slab", None, "hodlr"),
        check_vma=False,
    )
```

time: 171 us -> 162 us (0.947)
  Pallas kernels: 169 us -> 161 us
    pallas_call x1, Pallas kernels: 169 us -> 161 us  [local(): pl.pallas_call(functools.partial(kernel, slabs, whole), out_shape=jax.Sha...]
where the time goes in v2:
time: 162 us
  Pallas kernels  161 us (99%)
    pallas_call x1, Pallas kernels, local(): pl.pallas_call(functools.partial(kernel, slabs, whole), out_shape=jax.Sha...  161 us

profile of v2, /device:TPU:231, one launch (start us, length us, event | category | flops | bytes accessed | tf_op | source)
XLA Modules:
  0.0 162.3 jit_solution(2252424687786257366)
XLA Ops:
  0.0 160.7 %sweep.1 = bf16[4,8,2048]{2,1,0:T(8,128)(2,1)} custom-call(bf16[4,8,2048]{2,1,0:T(8,128)(2,1)} %bitcast.9, bf16[2,1024,1024]{2,1,0:T(8,128)(2,1)} %bitcast.5, bf16[256,2048]{1,0:T(8,128)(2,1)} %bitcast.6, bf16[256,2048]{1,0:T(8,128)(2,1)} %bitcast.7), custom_call_target="tpu_custom_call" | custom-call | tf_op jit(solution)/shard_map/sweep/pallas_call | solution.py:263
  160.7 1.6 copy.6

commit v3 on v2

--- a/solution.py
+++ b/solution.py
@@ -11,6 +11,7 @@
 GROUPS = 4
 WHOLE_SLABS = 4
 PEERS = 8
+ORDER = (4, 6, 5, 7, 2, 3, 1)
 
 
 def flipped(member, j):
@@ -81,28 +82,35 @@
     def greet(slab, member):
         pl.semaphore_signal(barrier, inc=1, device_id=(slab, member), device_id_type=MESH)
 
-    for j in range(1, PEERS):
-        greet(k, flipped(m, j))
-
-    @pl.when(k > 0)
+    @pl.when(own)
+    def _():
+        for j in range(1, PEERS):
+            greet(k, flipped(m, j))
+
+    @pl.when(whole_recv)
+    def _():
+        greet(k - 1, m)
+
+    @pl.when(whole_send)
+    def _():
+        greet(k + 1, m)
+
+    @pl.when(split_recv)
     def _():
         for j in range(PEERS):
             greet(k - 1, flipped(m, j))
 
-    @pl.when(k < slabs - 1)
+    @pl.when(split_send)
     def _():
         for j in range(PEERS):
             greet(k + 1, flipped(m, j))
 
-    edge = jnp.logical_or(first, last)
-
-    @pl.when(edge)
-    def _():
-        pl.semaphore_wait(barrier, 2 * PEERS - 1)
-
-    @pl.when(jnp.logical_not(edge))
-    def _():
-        pl.semaphore_wait(barrier, 3 * PEERS - 1)
+    met = (
+        jnp.where(own, PEERS - 1, 0)
+        + jnp.where(whole_recv, 1, 0) + jnp.where(whole_send, 1, 0)
+        + jnp.where(split_recv, PEERS, 0) + jnp.where(split_send, PEERS, 0)
+    )
+    pl.semaphore_wait(barrier, met)
 
     @pl.when(split_send)
     def _():
@@ -129,61 +137,87 @@
     def _():
         u_copy().wait_recv()
 
-    @pl.loop(0, groups)
-    def _(g):
-        @pl.when(first)
-        def _():
-            for i, cols in enumerate(halves):
-                w_buf[g, i] = src[g, :, cols]
-
-        @pl.when(whole_recv)
-        def _():
-            for i, cols in enumerate(halves):
-                l_copy(g, i).wait_recv()
-                w_buf[g, i] = (src[g, :, cols].astype(wide) + l_in[g, i].astype(wide)).astype(bf16)
-
-        @pl.when(split_recv)
-        def _():
-            for j in range(1, PEERS):
-                p_copy(g, j).wait_recv()
-            parts = low_rank(lambda j: p_in[g, j].astype(wide), u_prev)
-            for i, cols in enumerate(halves):
-                l_copy(g, i).wait_recv()
-                front = (l_in[g, i].astype(wide) + parts[i]).astype(bf16)
-                back[g, i] = front
-                w_buf[g, i] = (src[g, :, cols].astype(wide) + front.astype(wide)).astype(bf16)
-
+    def whole_in(g):
+        pieces = []
+        for i, cols in enumerate(halves):
+            l_copy(g, i).wait_recv()
+            pieces.append((src[g, :, cols].astype(wide) + l_in[g, i].astype(wide)).astype(bf16))
+        return pieces
+
+    def split_in(g):
+        for j in range(1, PEERS):
+            p_copy(g, j).wait_recv()
+        for i in range(nleaf):
+            l_copy(g, i).wait_recv()
+        parts = low_rank(lambda j: p_in[g, j].astype(wide), u_prev)
+        pieces = []
+        for i, cols in enumerate(halves):
+            front = (l_in[g, i].astype(wide) + parts[i]).astype(bf16)
+            back[g, i] = front
+            pieces.append((src[g, :, cols].astype(wide) + front.astype(wide)).astype(bf16))
+        return pieces
+
+    def project(g, w):
         inner = [
-            lax.dot_general(w_buf[g, i], v[:, cols], (((1,), (1,)), ((), ())), preferred_element_type=wide)
+            lax.dot_general(w[i], v[:, cols], (((1,), (1,)), ((), ())), preferred_element_type=wide)
             for i, cols in enumerate(halves)
         ]
         total = inner[0] + inner[1]
         p_send[g, 0] = total[:, :128].astype(bf16)
         p_send[g, 1] = total[:, 128:].astype(bf16)
-        for i in range(nleaf):
-            p_send[g, 2 + i] = jnp.where(low, 0.0, inner[1 - i][:, 128:]).astype(bf16)
-
-        @pl.when(split_send)
-        def _():
-            for j in (4, 6, 5, 7, 2, 3, 1):
-                p_copy(g, j).start()
-
-        @pl.when(own)
-        def _():
-            for j in (4, 6, 5, 7, 2, 3, 1):
+        return [jnp.where(low, 0.0, inner[1 - i][:, 128:]).astype(bf16) for i in range(nleaf)]
+
+    def split_out(g, w):
+        four = project(g, w)
+        for j in ORDER:
+            p_copy(g, j).start()
+        for i, cols in enumerate(halves):
+            part = jnp.dot(w[i], leaf[i], preferred_element_type=wide)
+            part += jnp.dot(four[i], u[cross - 64 :, cols], preferred_element_type=wide)
+            l_send[g, i] = part.astype(bf16)
+            l_copy(g, i).start()
+
+    @pl.when(jnp.logical_and(whole_recv, split_send))
+    def _():
+        @pl.loop(0, groups)
+        def _(g):
+            split_out(g, whole_in(g))
+
+    @pl.when(jnp.logical_and(split_recv, split_send))
+    def _():
+        @pl.loop(0, groups)
+        def _(g):
+            split_out(g, split_in(g))
+            back_copy(g).start()
+
+    @pl.when(own)
+    def _():
+        @pl.loop(0, groups)
+        def _(g):
+            def keep(pieces):
+                for i in range(nleaf):
+                    w_buf[g, i] = pieces[i]
+
+            @pl.when(first)
+            def _():
+                keep([src[g, :, cols] for cols in halves])
+
+            @pl.when(whole_recv)
+            def _():
+                keep(whole_in(g))
+
+            @pl.when(split_recv)
+            def _():
+                keep(split_in(g))
+
+            for i, piece in enumerate(project(g, [w_buf[g, i] for i in range(nleaf)])):
+                p_send[g, 2 + i] = piece
+            for j in ORDER:
                 q_copy(g, j).start()
 
-        @pl.when(split_send)
-        def _():
-            for i, cols in enumerate(halves):
-                part = jnp.dot(w_buf[g, i], leaf[i], preferred_element_type=wide)
-                part += jnp.dot(p_send[g, 2 + i], u[cross - 64 :, cols], preferred_element_type=wide)
-                l_send[g, i] = part.astype(bf16)
-                l_copy(g, i).start()
-
-        @pl.when(split_recv)
-        def _():
-            back_copy(g).start()
+            @pl.when(split_recv)
+            def _():
+                back_copy(g).start()
 
     @pl.when(first)
     def _():

time: 162 us -> 158 us (0.975)
  Pallas kernels: 161 us -> 156 us
    pallas_call x1, Pallas kernels: 161 us -> 156 us  [local(): pl.pallas_call(functools.partial(kernel, slabs, whole), out_shape=jax.Sha...]
where the time goes in v3:
time: 158 us
  Pallas kernels  156 us (99%)
    pallas_call x1, Pallas kernels, local(): pl.pallas_call(functools.partial(kernel, slabs, whole), out_shape=jax.Sha...  156 us

profile of v3, /device:TPU:231, one launch (start us, length us, event | category | flops | bytes accessed | tf_op | source)
XLA Modules:
  0.0 157.7 jit_solution(5944123074446644693)
XLA Ops:
  0.0 156.1 %sweep.1 = bf16[4,8,2048]{2,1,0:T(8,128)(2,1)} custom-call(bf16[4,8,2048]{2,1,0:T(8,128)(2,1)} %bitcast.9, bf16[2,1024,1024]{2,1,0:T(8,128)(2,1)} %bitcast.5, bf16[256,2048]{1,0:T(8,128)(2,1)} %bitcast.6, bf16[256,2048]{1,0:T(8,128)(2,1)} %bitcast.7), custom_call_target="tpu_custom_call" | custom-call | tf_op jit(solution)/shard_map/sweep/pallas_call | solution.py:297
  156.2 1.6 copy.6

commit v4 on v3

v4 whole, which is shorter than its diff:
```python
import functools

import jax
import jax.numpy as jnp
from jax import lax
from jax.experimental import pallas as pl
from jax.experimental.pallas import tpu as pltpu
from jax.sharding import PartitionSpec as P

MESH = pl.DeviceIdType.MESH
GROUPS = 4
WHOLE_SLABS = 4
PEERS = 8
CHUNKS = 1
ORDER = (4, 6, 5, 7, 2, 3, 1)


def flipped(member, j):
    bits = (lax.rem(member, 2), lax.rem(lax.div(member, 2), 2), lax.div(member, 4))
    total = 0
    for i, bit in enumerate(bits):
        total = total + (1 << i) * ((1 - bit) if (j >> i) & 1 else bit)
    return total


def kernel(
    slabs, whole, src_hbm, leaf_hbm, v_hbm, u_hbm, out,
    src, leaf, v, u, src_sem, leaf_sem, v_sem, u_sem, u_prev, mixed, w_buf, l_in, p_in, p_self, l_send, l_wide, p_send, back, back_in,
    u_ss, u_rs, l_ss, l_rs, p_ss, p_rs, q_ss, q_rs, b_ss, b_rs,
):
    k = lax.axis_index("slab")
    m = lax.axis_index("hodlr")
    groups, rows, width = src.shape
    nleaf, strips, size, _ = leaf.shape
    cross = u_prev.shape[1]
    bf16, wide = jnp.bfloat16, jnp.float32

    first, last = k == 0, k == slabs - 1
    whole_send = k + 1 < whole
    split_send = jnp.logical_and(k + 1 >= whole, k < slabs - 1)
    whole_recv = jnp.logical_and(k >= 1, k < whole)
    split_recv = k >= whole
    own = jnp.logical_or(whole_send, last)
    chunks, part_width = l_in.shape[1], l_in.shape[3]
    per_leaf, lanes = chunks // nleaf, part_width // 128
    spans = [slice(c * part_width, (c + 1) * part_width) for c in range(chunks)]

    def remote(source, target, send, recv, slab, member):
        return pltpu.make_async_remote_copy(
            src_ref=source, dst_ref=target, send_sem=send, recv_sem=recv,
            device_id=(slab, member), device_id_type=MESH,
        )

    def u_copy():
        return remote(u.at[:, pl.ds(0, cross)], u_prev, u_ss, u_rs, k + 1, m)

    def l_copy(g, i):
        return remote(l_send.at[g, i], l_in.at[g, i], l_ss.at[g, i], l_rs.at[g, i], k + 1, m)

    def back_copy(g):
        return remote(back.at[g], back_in.at[g], b_ss.at[g], b_rs.at[g], k - 1, m)

    def tile_of(j):
        return 1 if j == 1 else 0

    def p_copy(g, j):
        return remote(
            p_send.at[g, tile_of(j)], p_in.at[g, j], p_ss.at[g, j], p_rs.at[g, j], k + 1, flipped(m, j)
        )

    def q_copy(g, j):
        return remote(
            p_send.at[g, tile_of(j)], p_self.at[g, j], q_ss.at[g, j], q_rs.at[g, j], k, flipped(m, j)
        )

    def strip(source, target, t, sem):
        return pltpu.make_async_copy(source.at[:, pl.ds(t * 128, 128)], target.at[t], sem)

    loads = [
        [pltpu.make_async_copy(src_hbm, src, src_sem)],
        [strip(v_hbm, v, t, v_sem.at[t]) for t in range(nleaf * strips)],
        [strip(leaf_hbm.at[i], leaf.at[i], t, leaf_sem.at[i, t]) for i in range(nleaf) for t in range(strips)],
        [strip(u_hbm, u, t, u_sem.at[t]) for t in range(nleaf * strips)],
    ]

    def arrived(parts):
        for part in parts:
            for load in part:
                load.wait()

    def begin(parts):
        for part in parts:
            for load in part:
                load.start()

    begin(loads[:2])

    @pl.when(jnp.logical_not(first))
    def _():
        begin((loads[3], loads[2]))

    def joined(ref, c, *rows_of):
        return jnp.concatenate([ref[(c * lanes + t, *rows_of)] for t in range(lanes)], axis=1)

    def side(pieces, i):
        return jnp.concatenate(pieces[i * per_leaf : (i + 1) * per_leaf], axis=1)

    barrier = pltpu.get_barrier_semaphore()

    def greet(slab, member):
        pl.semaphore_signal(barrier, inc=1, device_id=(slab, member), device_id_type=MESH)

    @pl.when(own)
    def _():
        for j in range(1, PEERS):
            greet(k, flipped(m, j))

    @pl.when(whole_recv)
    def _():
        greet(k - 1, m)

    @pl.when(whole_send)
    def _():
        greet(k + 1, m)

    @pl.when(split_recv)
    def _():
        for j in range(PEERS):
            greet(k - 1, flipped(m, j))

    @pl.when(split_send)
    def _():
        for j in range(PEERS):
            greet(k + 1, flipped(m, j))

    met = (
        jnp.where(own, PEERS - 1, 0)
        + jnp.where(whole_recv, 1, 0) + jnp.where(whole_send, 1, 0)
        + jnp.where(split_recv, PEERS, 0) + jnp.where(split_send, PEERS, 0)
    )
    pl.semaphore_wait(barrier, met)

    @pl.when(split_send)
    def _():
        arrived(loads[3:])
        u_copy().start()

    low = lax.broadcasted_iota(jnp.int32, (rows, 128), 1) < 64

    def shared(read):
        one = read(4) + read(5) + read(6) + read(7)
        two = read(2) + read(3)
        top = jnp.where(low, one, two)
        return jnp.concatenate([top, read(1)], axis=1).astype(bf16)[:, :cross]

    def low_rank(both, factors):
        return [
            jnp.dot(both, joined(factors, c, slice(0, cross)), preferred_element_type=wide) for c in range(chunks)
        ]

    arrived(loads[:2])

    @pl.when(first)
    def _():
        begin(loads[2:])

    @pl.when(jnp.logical_not(first))
    def _():
        arrived(loads[2:3])

    @pl.when(split_recv)
    def _():
        u_copy().wait_recv()

    def added_to_source(g, c, front):
        return (src[g, :, spans[c]].astype(wide) + front.astype(wide)).astype(bf16)

    def whole_in(g):
        pieces = []
        for c in range(chunks):
            l_copy(g, c).wait_recv()
            pieces.append(added_to_source(g, c, l_in[g, c]))
        return pieces

    def completed(g, parts):
        pieces = []
        for c in range(chunks):
            front = (l_in[g, c].astype(wide) + parts[c]).astype(bf16)
            back[g, c] = front
            pieces.append(added_to_source(g, c, front))
        return pieces

    def split_in(g):
        for j in range(1, PEERS):
            p_copy(g, j).wait_recv()
        for c in range(chunks):
            l_copy(g, c).wait_recv()
        return completed(g, low_rank(shared(lambda j: p_in[g, j].astype(wide)), u_prev))

    def one_inner(piece, c):
        return lax.dot_general(piece, joined(v, c), (((1,), (1,)), ((), ())), preferred_element_type=wide)

    def inner_of(pieces):
        inner = []
        for i in range(nleaf):
            terms = [one_inner(pieces[c], c) for c in range(i * per_leaf, (i + 1) * per_leaf)]
            inner.append(functools.reduce(jnp.add, terms))
        return inner

    def project(g, pieces):
        inner = inner_of(pieces)
        total = inner[0] + inner[1]
        p_send[g, 0] = total[:, :128].astype(bf16)
        p_send[g, 1] = total[:, 128:].astype(bf16)
        return [jnp.where(low, 0.0, inner[1 - i][:, 128:]).astype(bf16) for i in range(nleaf)]

    def block_part(piece, four, c):
        i, first_strip = c // per_leaf, (c % per_leaf) * lanes
        factor = jnp.concatenate([leaf[i, first_strip + t] for t in range(lanes)], axis=1)
        part = jnp.dot(piece, factor, preferred_element_type=wide)
        return part + jnp.dot(four, joined(u, c, slice(cross - 64, None)), preferred_element_type=wide)

    def send_parts(g, pieces, four):
        for i in range(nleaf):
            piece = side(pieces, i)
            for c in range(i * per_leaf, (i + 1) * per_leaf):
                l_send[g, c] = block_part(piece, four[i], c).astype(bf16)
                l_copy(g, c).start()

    def split_out(g, pieces):
        four = project(g, pieces)
        for j in ORDER:
            p_copy(g, j).start()
        send_parts(g, pieces, four)

    @pl.when(jnp.logical_and(whole_recv, split_send))
    def _():
        @pl.loop(0, groups)
        def _(g):
            split_out(g, whole_in(g))

    @pl.when(k == whole)
    def _():
        @pl.loop(0, groups)
        def _(g):
            split_out(g, split_in(g))
            back_copy(g).start()

    @pl.when(jnp.logical_and(k > whole, split_send))
    def _():
        inner = inner_of([joined(u_prev, c) for c in range(chunks)])
        total = (inner[0] + inner[1]).astype(bf16)
        mixed[0] = total[:, :128]
        mixed[1] = total[:, 128:]
        mixed[2] = inner[1][:, 128:].astype(bf16)
        mixed[3] = inner[0][:, 128:].astype(bf16)

        @pl.loop(0, groups)
        def _(g):
            terms = []
            for c in range(chunks):
                l_copy(g, c).wait_recv()
                terms.append(one_inner(added_to_source(g, c, l_in[g, c]), c))
            base = [functools.reduce(jnp.add, terms[i * per_leaf : (i + 1) * per_leaf]) for i in range(nleaf)]
            ready = base[0] + base[1]
            for j in range(1, PEERS):
                p_copy(g, j).wait_recv()
            both = shared(lambda j: p_in[g, j].astype(wide))
            added = jnp.dot(both, jnp.concatenate([mixed[t] for t in range(4)], axis=1), preferred_element_type=wide)
            p_send[g, 0] = (ready[:, :128] + added[:, :128]).astype(bf16)
            p_send[g, 1] = (ready[:, 128:] + added[:, 128:256]).astype(bf16)
            for j in ORDER:
                p_copy(g, j).start()
            pieces = completed(g, low_rank(both, u_prev))
            four = []
            for i in range(nleaf):
                value = base[1 - i][:, 128:] + added[:, 256 + 128 * i : 384 + 128 * i]
                four.append(jnp.where(low, 0.0, value).astype(bf16))
            send_parts(g, pieces, four)
            back_copy(g).start()

    @pl.when(own)
    def _():
        @pl.loop(0, groups)
        def _(g):
            def keep(pieces):
                for c in range(chunks):
                    w_buf[g, c] = pieces[c]

            @pl.when(first)
            def _():
                keep([src[g, :, span] for span in spans])

            @pl.when(whole_recv)
            def _():
                keep(whole_in(g))

            @pl.when(split_recv)
            def _():
                keep(split_in(g))

            for i, piece in enumerate(project(g, [w_buf[g, c] for c in range(chunks)])):
                p_send[g, 2 + i] = piece
            for j in ORDER:
                q_copy(g, j).start()

            @pl.when(split_recv)
            def _():
                back_copy(g).start()

    @pl.when(first)
    def _():
        arrived(loads[2:3])

    @pl.when(own)
    def _():
        arrived(loads[3:])

    def stacked(array):
        return array.astype(wide).reshape(groups * rows, array.shape[-1]).astype(bf16)

    @pl.when(own)
    def _():
        for i in range(nleaf):
            piece = jnp.concatenate(
                [stacked(w_buf[:, c]) for c in range(i * per_leaf, (i + 1) * per_leaf)], axis=1
            )
            four = stacked(p_send[:, 2 + i])
            for c in range(i * per_leaf, (i + 1) * per_leaf):
                l_wide[:, c] = block_part(piece, four, c).reshape(groups, rows, part_width)

        @pl.loop(0, groups)
        def _(g):
            for j in range(1, PEERS):
                q_copy(g, j).wait_recv()
            parts = low_rank(shared(lambda j: p_self[g, j].astype(wide)), u)
            for c, span in enumerate(spans):
                front = (l_wide[g, c] + parts[c]).astype(bf16)
                out[g, :, span] = front
                l_send[g, c] = front

                @pl.when(whole_send)
                def _(c=c):
                    l_copy(g, c).start()

        @pl.loop(0, groups)
        def _(g):
            for j in range(1, PEERS):
                q_copy(g, j).wait_send()

            @pl.when(whole_send)
            def _():
                for c in range(chunks):
                    l_copy(g, c).wait_send()

    @pl.when(split_send)
    def _():
        u_copy().wait_send()

        @pl.loop(0, groups)
        def _(g):
            for c in range(chunks):
                l_copy(g, c).wait_send()
            for j in range(1, PEERS):
                p_copy(g, j).wait_send()
            back_copy(g).wait_recv()
            for c, span in enumerate(spans):
                out[g, :, span] = back_in[g, c]

    @pl.when(split_recv)
    def _():
        @pl.loop(0, groups)
        def _(g):
            back_copy(g).wait_send()


def solution(mesh, groups=GROUPS, whole=WHOLE_SLABS):
    slabs = mesh.shape["slab"]

    def local(sources, leaves, v_rows, u_rows):
        shots, width = sources.shape[1:]
        nleaf, size = leaves.shape[1:3]
        levels, rank = v_rows.shape[1:3]
        rows = shots // groups
        bf16, wide = jnp.bfloat16, jnp.float32
        dma = pltpu.SemaphoreType.DMA
        vmem = pl.BlockSpec(memory_space=pltpu.VMEM)

        def split(dtype):
            return pltpu.VMEM((groups, CHUNKS * nleaf, rows, size // CHUNKS), dtype)

        swept = pl.pallas_call(
            functools.partial(kernel, slabs, whole),
            out_shape=jax.ShapeDtypeStruct((groups, rows, width), bf16),
            in_specs=[pl.BlockSpec(memory_space=pl.ANY)] * 4,
            out_specs=vmem,
            scratch_shapes=[
                pltpu.VMEM((groups, rows, width), bf16),
                pltpu.VMEM((nleaf, size // 128, size, 128), bf16),
                pltpu.VMEM((width // 128, levels * rank, 128), bf16),
                pltpu.VMEM((width // 128, levels * rank, 128), bf16),
                dma, dma((nleaf, size // 128)), dma((width // 128,)), dma((width // 128,)),
                pltpu.VMEM((width // 128, (levels - 1) * rank, 128), bf16),
                pltpu.VMEM((4, (levels - 1) * rank, 128), bf16),
                split(bf16),
                split(bf16),
                pltpu.VMEM((groups, PEERS, rows, 128), bf16),
                pltpu.VMEM((groups, PEERS, rows, 128), bf16),
                split(bf16),
                split(wide),
                pltpu.VMEM((groups, 2 + nleaf, rows, 128), bf16),
                split(bf16),
                split(bf16),
                dma, dma,
                dma((groups, CHUNKS * nleaf)), dma((groups, CHUNKS * nleaf)),
                dma((groups, PEERS)), dma((groups, PEERS)),
                dma((groups, PEERS)), dma((groups, PEERS)),
                dma((groups,)), dma((groups,)),
            ],
            compiler_params=pltpu.CompilerParams(collective_id=0, has_side_effects=True),
            name="sweep",
        )(
            sources[0].reshape(groups, rows, width),
            leaves[0],
            v_rows[0].reshape(levels * rank, width),
            u_rows[0].reshape(levels * rank, width),
        )
        return swept.reshape(1, shots, width)

    return jax.shard_map(
        local,
        mesh=mesh,
        in_specs=(
            P("slab", None, "hodlr"),
            P("slab", "hodlr", None, None),
            P("slab", None, None, "hodlr"),
            P("slab", None, None, "hodlr"),
        ),
        out_specs=P("slab", None, "hodlr"),
        check_vma=False,
    )
```

time: 158 us -> 154 us (0.975)
  Pallas kernels: 156 us -> 153 us
    pallas_call x1, Pallas kernels: 156 us -> 153 us  [local(): pl.pallas_call(functools.partial(kernel, slabs, whole), out_shape=jax.Sha...]
where the time goes in v4:
time: 154 us
  Pallas kernels  153 us (99%)
  local copies, waits for them, and re-layouts  1.57 us (1%)
    pallas_call x1, Pallas kernels, local(): pl.pallas_call(functools.partial(kernel, slabs, whole), out_shape=jax.Sha...  153 us

profile of v4, /device:TPU:231, one launch (start us, length us, event | category | flops | bytes accessed | tf_op | source)
XLA Modules:
  0.0 154.1 jit_solution(15345963351031665186)
XLA Ops:
  0.0 152.5 %sweep.1 = bf16[4,8,2048]{2,1,0:T(8,128)(2,1)} custom-call(bf16[4,8,2048]{2,1,0:T(8,128)(2,1)} %bitcast.9, bf16[2,1024,1024]{2,1,0:T(8,128)(2,1)} %bitcast.5, bf16[256,2048]{1,0:T(8,128)(2,1)} %bitcast.6, bf16[256,2048]{1,0:T(8,128)(2,1)} %bitcast.7), custom_call_target="tpu_custom_call" | custom-call | tf_op jit(solution)/shard_map/sweep/pallas_call | solution.py:392
  152.5 1.6 %copy.6 = bf16[1,32,2048]{2,1,0:T(8,128)(2,1)} copy(bf16[1,32,2048]{2,1,0:T(8,128)(2,1)} %bitcast.8) | data formatting | bytes 262144

commit v5 on v4

--- a/solution.py
+++ b/solution.py
@@ -133,18 +133,6 @@
         for j in range(PEERS):
             greet(k + 1, flipped(m, j))
 
-    met = (
-        jnp.where(own, PEERS - 1, 0)
-        + jnp.where(whole_recv, 1, 0) + jnp.where(whole_send, 1, 0)
-        + jnp.where(split_recv, PEERS, 0) + jnp.where(split_send, PEERS, 0)
-    )
-    pl.semaphore_wait(barrier, met)
-
-    @pl.when(split_send)
-    def _():
-        arrived(loads[3:])
-        u_copy().start()
-
     low = lax.broadcasted_iota(jnp.int32, (rows, 128), 1) < 64
 
     def shared(read):
@@ -158,19 +146,6 @@
             jnp.dot(both, joined(factors, c, slice(0, cross)), preferred_element_type=wide) for c in range(chunks)
         ]
 
-    arrived(loads[:2])
-
-    @pl.when(first)
-    def _():
-        begin(loads[2:])
-
-    @pl.when(jnp.logical_not(first))
-    def _():
-        arrived(loads[2:3])
-
-    @pl.when(split_recv)
-    def _():
-        u_copy().wait_recv()
 
     def added_to_source(g, c, front):
         return (src[g, :, spans[c]].astype(wide) + front.astype(wide)).astype(bf16)
@@ -233,6 +208,31 @@
             p_copy(g, j).start()
         send_parts(g, pieces, four)
 
+    @pl.when(first)
+    def _():
+        arrived(loads[:2])
+        begin(loads[2:])
+
+    met = (
+        jnp.where(own, PEERS - 1, 0)
+        + jnp.where(whole_recv, 1, 0) + jnp.where(whole_send, 1, 0)
+        + jnp.where(split_recv, PEERS, 0) + jnp.where(split_send, PEERS, 0)
+    )
+    pl.semaphore_wait(barrier, met)
+
+    @pl.when(split_send)
+    def _():
+        arrived(loads[3:])
+        u_copy().start()
+
+    @pl.when(jnp.logical_not(first))
+    def _():
+        arrived(loads[:3])
+
+    @pl.when(split_recv)
+    def _():
+        u_copy().wait_recv()
+
     @pl.when(jnp.logical_and(whole_recv, split_send))
     def _():
         @pl.loop(0, groups)
@@ -246,7 +246,29 @@
             split_out(g, split_in(g))
             back_copy(g).start()
 
-    @pl.when(jnp.logical_and(k > whole, split_send))
+    def mixed_projection(g):
+        terms = []
+        for c in range(chunks):
+            l_copy(g, c).wait_recv()
+            terms.append(one_inner(added_to_source(g, c, l_in[g, c]), c))
+        base = [functools.reduce(jnp.add, terms[i * per_leaf : (i + 1) * per_leaf]) for i in range(nleaf)]
+        ready = base[0] + base[1]
+        for j in range(1, PEERS):
+            p_copy(g, j).wait_recv()
+        both = shared(lambda j: p_in[g, j].astype(wide))
+        added = jnp.dot(both, jnp.concatenate([mixed[t] for t in range(4)], axis=1), preferred_element_type=wide)
+        p_send[g, 0] = (ready[:, :128] + added[:, :128]).astype(bf16)
+        p_send[g, 1] = (ready[:, 128:] + added[:, 128:256]).astype(bf16)
+        return base, added, both
+
+    def mixed_four(base, added):
+        four = []
+        for i in range(nleaf):
+            value = base[1 - i][:, 128:] + added[:, 256 + 128 * i : 384 + 128 * i]
+            four.append(jnp.where(low, 0.0, value).astype(bf16))
+        return four
+
+    @pl.when(k > whole)
     def _():
         inner = inner_of([joined(u_prev, c) for c in range(chunks)])
         total = (inner[0] + inner[1]).astype(bf16)
@@ -255,58 +277,54 @@
         mixed[2] = inner[1][:, 128:].astype(bf16)
         mixed[3] = inner[0][:, 128:].astype(bf16)
 
-        @pl.loop(0, groups)
-        def _(g):
-            terms = []
-            for c in range(chunks):
-                l_copy(g, c).wait_recv()
-                terms.append(one_inner(added_to_source(g, c, l_in[g, c]), c))
-            base = [functools.reduce(jnp.add, terms[i * per_leaf : (i + 1) * per_leaf]) for i in range(nleaf)]
-            ready = base[0] + base[1]
-            for j in range(1, PEERS):
-                p_copy(g, j).wait_recv()
-            both = shared(lambda j: p_in[g, j].astype(wide))
-            added = jnp.dot(both, jnp.concatenate([mixed[t] for t in range(4)], axis=1), preferred_element_type=wide)
-            p_send[g, 0] = (ready[:, :128] + added[:, :128]).astype(bf16)
-            p_send[g, 1] = (ready[:, 128:] + added[:, 128:256]).astype(bf16)
+    @pl.when(jnp.logical_and(k > whole, split_send))
+    def _():
+        @pl.loop(0, groups)
+        def _(g):
+            base, added, both = mixed_projection(g)
             for j in ORDER:
                 p_copy(g, j).start()
             pieces = completed(g, low_rank(both, u_prev))
-            four = []
-            for i in range(nleaf):
-                value = base[1 - i][:, 128:] + added[:, 256 + 128 * i : 384 + 128 * i]
-                four.append(jnp.where(low, 0.0, value).astype(bf16))
-            send_parts(g, pieces, four)
+            send_parts(g, pieces, mixed_four(base, added))
             back_copy(g).start()
 
-    @pl.when(own)
-    def _():
-        @pl.loop(0, groups)
-        def _(g):
-            def keep(pieces):
-                for c in range(chunks):
-                    w_buf[g, c] = pieces[c]
-
-            @pl.when(first)
-            def _():
-                keep([src[g, :, span] for span in spans])
-
-            @pl.when(whole_recv)
-            def _():
-                keep(whole_in(g))
-
-            @pl.when(split_recv)
-            def _():
-                keep(split_in(g))
-
-            for i, piece in enumerate(project(g, [w_buf[g, c] for c in range(chunks)])):
+    @pl.when(first)
+    def _():
+        @pl.loop(0, groups)
+        def _(g):
+            pieces = [src[g, :, span] for span in spans]
+            for i, piece in enumerate(project(g, pieces)):
                 p_send[g, 2 + i] = piece
             for j in ORDER:
                 q_copy(g, j).start()
-
-            @pl.when(split_recv)
-            def _():
-                back_copy(g).start()
+            for c in range(chunks):
+                w_buf[g, c] = pieces[c]
+
+    @pl.when(jnp.logical_and(whole_recv, whole_send))
+    def _():
+        @pl.loop(0, groups)
+        def _(g):
+            pieces = whole_in(g)
+            for i, piece in enumerate(project(g, pieces)):
+                p_send[g, 2 + i] = piece
+            for j in ORDER:
+                q_copy(g, j).start()
+            for c in range(chunks):
+                w_buf[g, c] = pieces[c]
+
+    @pl.when(last)
+    def _():
+        @pl.loop(0, groups)
+        def _(g):
+            base, added, both = mixed_projection(g)
+            for j in ORDER:
+                q_copy(g, j).start()
+            pieces = completed(g, low_rank(both, u_prev))
+            back_copy(g).start()
+            for c in range(chunks):
+                w_buf[g, c] = pieces[c]
+            for i, piece in enumerate(mixed_four(base, added)):
+                p_send[g, 2 + i] = piece
 
     @pl.when(first)
     def _():
@@ -391,7 +409,7 @@
 
         swept = pl.pallas_call(
             functools.partial(kernel, slabs, whole),
-            out_shape=jax.ShapeDtypeStruct((groups, rows, width), bf16),
+            out_shape=pltpu.VMEM((groups, rows, width), bf16),
             in_specs=[pl.BlockSpec(memory_space=pl.ANY)] * 4,
             out_specs=vmem,
             scratch_shapes=[

time: 154 us -> 152 us (0.987)
  no operation moved by 1% of the time
where the time goes in v5:
time: 152 us
  Pallas kernels  152 us (100%)
    pallas_call x1, Pallas kernels, local(): pl.pallas_call(functools.partial(kernel, slabs, whole), out_shape=pltpu.V...  152 us

profile of v5, /device:TPU:231, one launch (start us, length us, event | category | flops | bytes accessed | tf_op | source)
XLA Modules:
  0.0 152.4 jit_solution(17405162151369462213)
XLA Ops:
  0.0 151.7 %sweep.1 = bf16[4,8,2048]{2,1,0:T(8,128)(2,1)S(1)} custom-call(bf16[4,8,2048]{2,1,0:T(8,128)(2,1)} %bitcast.9, bf16[2,1024,1024]{2,1,0:T(8,128)(2,1)} %bitcast.6, bf16[256,2048]{1,0:T(8,128)(2,1)} %bitcast.7, bf16[256,2048]{1,0:T(8,128)(2,1)} %bitcast.8), custom_call_target="tpu_custom_call" | custom-call | tf_op jit(solution)/shard_map/sweep/pallas_call | solution.py:410
  151.7 0.7 copy.6

commit v6 on v5

--- a/solution.py
+++ b/solution.py
@@ -9,7 +9,7 @@
 
 MESH = pl.DeviceIdType.MESH
 GROUPS = 4
-WHOLE_SLABS = 4
+WHOLE_SLABS = 3
 PEERS = 8
 CHUNKS = 1
 ORDER = (4, 6, 5, 7, 2, 3, 1)
@@ -41,6 +41,10 @@
     whole_recv = jnp.logical_and(k >= 1, k < whole)
     split_recv = k >= whole
     own = jnp.logical_or(whole_send, last)
+    near_send = jnp.logical_or(k == whole - 1, k == whole)
+    near_recv = jnp.logical_or(k == whole, k == whole + 1)
+    far_send = jnp.logical_and(k > whole, k < slabs - 1)
+    far_recv = k > whole + 1
     chunks, part_width = l_in.shape[1], l_in.shape[3]
     per_leaf, lanes = chunks // nleaf, part_width // 128
     spans = [slice(c * part_width, (c + 1) * part_width) for c in range(chunks)]
@@ -51,8 +55,8 @@
             device_id=(slab, member), device_id_type=MESH,
         )
 
-    def u_copy():
-        return remote(u.at[:, pl.ds(0, cross)], u_prev, u_ss, u_rs, k + 1, m)
+    def u_copy(height):
+        return remote(u.at[:, pl.ds(0, height)], u_prev.at[:, pl.ds(0, height)], u_ss, u_rs, k + 1, m)
 
     def l_copy(g, i):
         return remote(l_send.at[g, i], l_in.at[g, i], l_ss.at[g, i], l_rs.at[g, i], k + 1, m)
@@ -115,6 +119,10 @@
         for j in range(1, PEERS):
             greet(k, flipped(m, j))
 
+    @pl.when(near_send)
+    def _():
+        greet(k, flipped(m, 1))
+
     @pl.when(whole_recv)
     def _():
         greet(k - 1, m)
@@ -135,15 +143,15 @@
 
     low = lax.broadcasted_iota(jnp.int32, (rows, 128), 1) < 64
 
+    def upper(read):
+        return jnp.where(low, read(4) + read(5) + read(6) + read(7), read(2) + read(3))
+
     def shared(read):
-        one = read(4) + read(5) + read(6) + read(7)
-        two = read(2) + read(3)
-        top = jnp.where(low, one, two)
-        return jnp.concatenate([top, read(1)], axis=1).astype(bf16)[:, :cross]
+        return jnp.concatenate([upper(read), read(1)], axis=1).astype(bf16)[:, :cross]
 
     def low_rank(both, factors):
         return [
-            jnp.dot(both, joined(factors, c, slice(0, cross)), preferred_element_type=wide) for c in range(chunks)
+            jnp.dot(both, joined(factors, c, slice(0, both.shape[1])), preferred_element_type=wide) for c in range(chunks)
         ]
 
 
@@ -165,12 +173,12 @@
             pieces.append(added_to_source(g, c, front))
         return pieces
 
-    def split_in(g):
-        for j in range(1, PEERS):
+    def near_in(g):
+        for j in range(2, PEERS):
             p_copy(g, j).wait_recv()
         for c in range(chunks):
             l_copy(g, c).wait_recv()
-        return completed(g, low_rank(shared(lambda j: p_in[g, j].astype(wide)), u_prev))
+        return completed(g, low_rank(upper(lambda j: p_in[g, j].astype(wide)).astype(bf16), u_prev))
 
     def one_inner(piece, c):
         return lax.dot_general(piece, joined(v, c), (((1,), (1,)), ((), ())), preferred_element_type=wide)
@@ -189,11 +197,16 @@
         p_send[g, 1] = total[:, 128:].astype(bf16)
         return [jnp.where(low, 0.0, inner[1 - i][:, 128:]).astype(bf16) for i in range(nleaf)]
 
-    def block_part(piece, four, c):
+    def leaf_part(piece, c):
         i, first_strip = c // per_leaf, (c % per_leaf) * lanes
         factor = jnp.concatenate([leaf[i, first_strip + t] for t in range(lanes)], axis=1)
-        part = jnp.dot(piece, factor, preferred_element_type=wide)
-        return part + jnp.dot(four, joined(u, c, slice(cross - 64, None)), preferred_element_type=wide)
+        return jnp.dot(piece, factor, preferred_element_type=wide)
+
+    def four_part(four, c):
+        return jnp.dot(four, joined(u, c, slice(cross - 64, None)), preferred_element_type=wide)
+
+    def block_part(piece, four, c):
+        return leaf_part(piece, c) + four_part(four, c)
 
     def send_parts(g, pieces, four):
         for i in range(nleaf):
@@ -214,7 +227,7 @@
         begin(loads[2:])
 
     met = (
-        jnp.where(own, PEERS - 1, 0)
+        jnp.where(own, PEERS - 1, 0) + jnp.where(near_send, 1, 0)
         + jnp.where(whole_recv, 1, 0) + jnp.where(whole_send, 1, 0)
         + jnp.where(split_recv, PEERS, 0) + jnp.where(split_send, PEERS, 0)
     )
@@ -223,27 +236,60 @@
     @pl.when(split_send)
     def _():
         arrived(loads[3:])
-        u_copy().start()
+
+    @pl.when(near_send)
+    def _():
+        u_copy(128).start()
+
+    @pl.when(far_send)
+    def _():
+        u_copy(cross).start()
 
     @pl.when(jnp.logical_not(first))
     def _():
         arrived(loads[:3])
 
-    @pl.when(split_recv)
-    def _():
-        u_copy().wait_recv()
-
-    @pl.when(jnp.logical_and(whole_recv, split_send))
-    def _():
-        @pl.loop(0, groups)
-        def _(g):
-            split_out(g, whole_in(g))
+    @pl.when(near_recv)
+    def _():
+        u_copy(128).wait_recv()
+
+    @pl.when(far_recv)
+    def _():
+        u_copy(cross).wait_recv()
+
+    def near_out(g, pieces):
+        four = project(g, pieces)
+        for j in ORDER[:-1]:
+            p_copy(g, j).start()
+        q_copy(g, 1).start()
+        for i in range(nleaf):
+            p_send[g, 2 + i] = four[i]
+        for c in range(chunks):
+            l_wide[g, c] = leaf_part(side(pieces, c // per_leaf), c)
+        q_copy(g, 1).wait_recv()
+        for c in range(chunks):
+            tile = jnp.where(low, p_self[g, 1].astype(wide), p_send[g, 2 + c // per_leaf].astype(wide)).astype(bf16)
+            l_send[g, c] = (l_wide[g, c] + four_part(tile, c)).astype(bf16)
+            l_copy(g, c).start()
+
+    @pl.when(jnp.logical_and(whole_recv, near_send))
+    def _():
+        @pl.loop(0, groups)
+        def _(g):
+            near_out(g, whole_in(g))
 
     @pl.when(k == whole)
     def _():
         @pl.loop(0, groups)
         def _(g):
-            split_out(g, split_in(g))
+            near_out(g, near_in(g))
+            back_copy(g).start()
+
+    @pl.when(k == whole + 1)
+    def _():
+        @pl.loop(0, groups)
+        def _(g):
+            split_out(g, near_in(g))
             back_copy(g).start()
 
     def mixed_projection(g):
@@ -268,7 +314,7 @@
             four.append(jnp.where(low, 0.0, value).astype(bf16))
         return four
 
-    @pl.when(k > whole)
+    @pl.when(far_recv)
     def _():
         inner = inner_of([joined(u_prev, c) for c in range(chunks)])
         total = (inner[0] + inner[1]).astype(bf16)
@@ -277,7 +323,7 @@
         mixed[2] = inner[1][:, 128:].astype(bf16)
         mixed[3] = inner[0][:, 128:].astype(bf16)
 
-    @pl.when(jnp.logical_and(k > whole, split_send))
+    @pl.when(jnp.logical_and(far_recv, split_send))
     def _():
         @pl.loop(0, groups)
         def _(g):
@@ -373,13 +419,27 @@
 
     @pl.when(split_send)
     def _():
-        u_copy().wait_send()
+        @pl.when(near_send)
+        def _():
+            u_copy(128).wait_send()
+
+            @pl.loop(0, groups)
+            def _(g):
+                q_copy(g, 1).wait_send()
+
+        @pl.when(far_send)
+        def _():
+            u_copy(cross).wait_send()
+
+            @pl.loop(0, groups)
+            def _(g):
+                p_copy(g, 1).wait_send()
 
         @pl.loop(0, groups)
         def _(g):
             for c in range(chunks):
                 l_copy(g, c).wait_send()
-            for j in range(1, PEERS):
+            for j in range(2, PEERS):
                 p_copy(g, j).wait_send()
             back_copy(g).wait_recv()
             for c, span in enumerate(spans):

time: 152 us -> 150 us (0.987)
  Pallas kernels: 152 us -> 149 us
    pallas_call x1, Pallas kernels: 152 us -> 149 us  [local(): pl.pallas_call(functools.partial(kernel, slabs, whole), out_shape=pltpu.V...]
where the time goes in v6:
time: 150 us
  Pallas kernels  149 us (99%)
    pallas_call x1, Pallas kernels, local(): pl.pallas_call(functools.partial(kernel, slabs, whole), out_shape=pltpu.V...  149 us

profile of v6, /device:TPU:231, one launch (start us, length us, event | category | flops | bytes accessed | tf_op | source)
XLA Modules:
  0.0 149.7 jit_solution(5215848693879630122)
XLA Ops:
  0.0 149.0 %sweep.1 = bf16[4,8,2048]{2,1,0:T(8,128)(2,1)S(1)} custom-call(bf16[4,8,2048]{2,1,0:T(8,128)(2,1)} %bitcast.9, bf16[2,1024,1024]{2,1,0:T(8,128)(2,1)} %bitcast.6, bf16[256,2048]{1,0:T(8,128)(2,1)} %bitcast.7, bf16[256,2048]{1,0:T(8,128)(2,1)} %bitcast.8), custom_call_target="tpu_custom_call" | custom-call | tf_op jit(solution)/shard_map/sweep/pallas_call | solution.py:470
  149.0 0.7 copy.6

commit v7 on v6

--- a/solution.py
+++ b/solution.py
@@ -97,12 +97,6 @@
             for load in part:
                 load.start()
 
-    begin(loads[:2])
-
-    @pl.when(jnp.logical_not(first))
-    def _():
-        begin((loads[3], loads[2]))
-
     def joined(ref, c, *rows_of):
         return jnp.concatenate([ref[(c * lanes + t, *rows_of)] for t in range(lanes)], axis=1)
 
@@ -116,7 +110,7 @@
 
     @pl.when(own)
     def _():
-        for j in range(1, PEERS):
+        for j in ORDER:
             greet(k, flipped(m, j))
 
     @pl.when(near_send)
@@ -140,6 +134,12 @@
     def _():
         for j in range(PEERS):
             greet(k + 1, flipped(m, j))
+
+    begin(loads[:2])
+
+    @pl.when(jnp.logical_not(first))
+    def _():
+        begin((loads[3], loads[2]))
 
     low = lax.broadcasted_iota(jnp.int32, (rows, 128), 1) < 64
 

time: 150 us -> 150 us (level)
  no operation moved by 1% of the time
where the time goes in v7:
time: 150 us
  Pallas kernels  149 us (99%)
    pallas_call x1, Pallas kernels, local(): pl.pallas_call(functools.partial(kernel, slabs, whole), out_shape=pltpu.V...  149 us

profile of v7, /device:TPU:231, one launch (start us, length us, event | category | flops | bytes accessed | tf_op | source)
XLA Modules:
  0.0 149.5 jit_solution(15359884373496381454)
XLA Ops:
  0.0 148.9 %sweep.1 = bf16[4,8,2048]{2,1,0:T(8,128)(2,1)S(1)} custom-call(bf16[4,8,2048]{2,1,0:T(8,128)(2,1)} %bitcast.9, bf16[2,1024,1024]{2,1,0:T(8,128)(2,1)} %bitcast.6, bf16[256,2048]{1,0:T(8,128)(2,1)} %bitcast.7, bf16[256,2048]{1,0:T(8,128)(2,1)} %bitcast.8), custom_call_target="tpu_custom_call" | custom-call | tf_op jit(solution)/shard_map/sweep/pallas_call | solution.py:470
  148.9 0.7 copy.6
